TPU v7x, 32 devices: a whole 2x2x4 slice. The times are simulated.
32 devices in a mesh: segment: 2 (over core), expert: 16 (over z, y, x).
Axes of the slice: x: 2, y: 2, z: 4, core: 2. Of those that a mesh axis runs over, the one named last changes fastest.
Arguments:
- rollout: bfloat16 [2048, 4096], P('expert', 'segment'), may hold values from -6 to 6
- norm_gain: bfloat16 [2, 4096], P('segment'), may hold values from 0.25 to 1.75
- router_first: bfloat16 [2, 4096, 28], P('segment')
- gain_second: bfloat16 [2, 4096], P('segment'), may hold values from 0.25 to 1.75
- router_second: bfloat16 [2, 4096, 28], P('segment')
- expert_ids: int32 [2048, 8], P('expert'), may hold values from 0 to 27, as said below
- copy_pick: int32 [2048, 8], P('expert'), may hold values from 0 to 5
- later_ids: int32 [2048, 8], P('expert'), may hold values from 0 to 27, all different within a row
- slot_table: int32 [32], replicated, may hold values from 0 to 27, as said below
- expert_in: bfloat16 [32, 4096, 1536], P(('segment', 'expert'))
- expert_out: bfloat16 [32, 768, 4096], P(('segment', 'expert'))
Outputs:
- states: bfloat16 [2, 2048, 4096], P('segment', 'expert')
- log_ratio: float32 [1024, 2], P('expert', 'segment')
Inputs may be any that keep to these rules, and one draw needn't show every extreme that they name: `expert_ids`: each row names 8 different experts. `slot_table`: every expert is held by one, two or three slots.
All inputs are finite; a program needn't handle non-finite values.
Results may differ from a plain program's by a relative error of at most 0.013.
The roundings to bfloat16 on the way count: a program that leaves them out, or rounds other values in their place, can miss the bound.
Values may be sent and summed in bfloat16 or wider, within the bound.
A program may use at most 192 MiB of HBM per device.

v0:
```python
import jax
import jax.numpy as jnp
from jax import lax
from jax.sharding import PartitionSpec as P


def partner_2(x, axis, apart):
    return lax.ppermute(x, axis, [(i, i ^ 1 << apart) for i in range(lax.axis_size(axis))])


def rms_scale(values, gain):
    return (
        values
        * lax.rsqrt(jnp.mean(values * values, axis=-1, keepdims=True) + 1e-06)
        * gain.astype(jnp.float32)
    )


def per_device(
    rollout,
    norm_gain,
    router_first,
    gain_second,
    router_second,
    expert_ids,
    copy_pick,
    later_ids,
    slot_table,
    expert_in,
    expert_out,
):
    whole = lax.all_gather(rollout, "segment", axis=1, tiled=True)
    tok_rows, width = whole.shape
    top_count = expert_ids.shape[1]
    experts_all = router_first.shape[2]
    slot_count = slot_table.shape[0]
    segment_count = lax.axis_size("segment")
    chip_count = lax.axis_size("expert")
    capacity = 3 * tok_rows * top_count // (2 * segment_count * chip_count)
    hidden_units = expert_out.shape[1]
    states_in = whole.astype(jnp.float32)
    normed = rms_scale(states_in, norm_gain[0]).astype(jnp.bfloat16)
    logits = jnp.dot(normed, router_first[0], preferred_element_type=jnp.float32)
    expert_cols = jnp.arange(experts_all, dtype=jnp.int32)
    picked = expert_ids[..., None] == expert_cols
    chosen = jnp.sum(jnp.where(picked, logits[:, None, :], 0.0), axis=-1)
    lifted = jnp.exp(chosen - jnp.max(chosen, axis=1, keepdims=True))
    gates = (lifted / jnp.sum(lifted, axis=1, keepdims=True)).astype(jnp.bfloat16)
    slot_ids = jnp.arange(slot_count, dtype=jnp.int32)
    same = slot_table[:, None] == slot_table[None, :]
    earlier = slot_ids[:, None] < slot_ids[None, :]
    copy_rank = jnp.sum((same & earlier).astype(jnp.int32), axis=0)
    holders = jnp.sum((slot_table[None, :] == expert_cols[:, None]).astype(jnp.int32), axis=1)
    copies = jnp.sum(picked.astype(jnp.int32) * holders, axis=-1)
    wanted = copy_pick % copies
    match = ((slot_table == expert_ids[..., None]) & (copy_rank == wanted[..., None])).astype(
        jnp.int32
    )
    slot = jnp.sum(match * slot_ids, axis=-1)
    flat = match.reshape(tok_rows * top_count, slot_count)
    before = jnp.cumsum(flat, axis=0) - flat
    rank = jnp.sum(before * flat, axis=-1).reshape(tok_rows, top_count)
    target = jnp.where(rank < capacity, slot * capacity + rank, -1)
    places = jnp.arange(slot_count * capacity, dtype=jnp.int32)
    hits = target[..., None] == places
    placing = jnp.sum(hits.astype(jnp.bfloat16), axis=1)
    outbound = jnp.einsum("tj,td->jd", placing, normed, preferred_element_type=jnp.float32)
    outbound = outbound.astype(jnp.bfloat16).reshape(slot_count, capacity, width)
    arrived = lax.all_to_all(
        outbound, ("segment", "expert"), split_axis=0, concat_axis=0, tiled=True
    )
    rows = arrived.reshape(-1, width)
    hidden = jnp.dot(rows, expert_in[0], preferred_element_type=jnp.float32)
    active = (jax.nn.silu(hidden[:, :hidden_units]) * hidden[:, hidden_units:]).astype(jnp.bfloat16)
    result = jnp.dot(active, expert_out[0], preferred_element_type=jnp.float32).astype(jnp.bfloat16)
    returned = lax.all_to_all(
        result.reshape(arrived.shape),
        ("segment", "expert"),
        split_axis=0,
        concat_axis=0,
        tiled=True,
    )
    returned = returned.reshape(slot_count * capacity, width)
    weights = jnp.sum(jnp.where(hits, gates.astype(jnp.float32)[..., None], 0.0), axis=1).astype(
        jnp.bfloat16
    )
    mixed = states_in + jnp.dot(weights, returned, preferred_element_type=jnp.float32)
    later = rms_scale(mixed, gain_second[0]).astype(jnp.bfloat16)
    logp = jax.nn.log_softmax(
        jnp.dot(later, router_second[0], preferred_element_type=jnp.float32), axis=-1
    )
    later_pick = later_ids[..., None] == expert_cols
    score = jnp.sum(jnp.where(later_pick, logp[:, None, :], 0.0), axis=(1, 2))
    partner = partner_2(score, "segment", 0)
    position = lax.axis_index("segment")
    ratio = jnp.where(position == 1, score - partner, partner - score)
    paired = ratio.reshape(tok_rows // 2, 2)
    mine = lax.dynamic_slice_in_dim(paired, position, 1, 1)
    return (mixed.astype(jnp.bfloat16)[None], mine)


def solution(mesh):
    in_specs = (
        P("expert", "segment"),
        P("segment", None),
        P("segment", None, None),
        P("segment", None),
        P("segment", None, None),
        P("expert", None),
        P("expert", None),
        P("expert", None),
        P(),
        P(("segment", "expert"), None, None),
        P(("segment", "expert"), None, None),
    )
    out_specs = (P("segment", "expert", None), P("expert", "segment"))
    return jax.shard_map(
        per_device, mesh=mesh, in_specs=in_specs, out_specs=out_specs, check_vma=False
    )
```

profile of v0, /device:TPU:0, one launch (start us, length us, event | category | flops | bytes accessed | tf_op | source)
XLA Modules:
  0.0 657.7 jit_solution(13061640426792384125)
XLA Ops:
  7.2 0.0 copy-start
  7.2 0.0 all-gather.2.cloned.1.call-start
  7.2 0.7 all-gather.2.cloned.1.call-update
  7.9 0.8 convert_reduce_fusion
  8.7 0.8 convert_reduce_fusion.1
  9.5 0.8 copy.33
  10.3 0.8 select_reduce_fusion.4
  11.1 0.8 add_select_fusion
  11.9 0.1 copy.34
  12.0 0.1 eq.159
  12.1 0.1 eq.151
  12.2 0.1 eq.155
  12.3 0.1 eq.137
  12.4 0.8 and_convert_fusion
  13.2 9.0 %reduce-window.6 = s32[32,8,128]{2,1,0:T(8,128)S(1)} reduce-window(s32[32,8,128]{2,1,0:T(8,128)S(1)} %and_convert_fusion, s32[]{:T(128)} %constant.20.clone.1), window={size=1x1x128 pad=0_0x0_0x127_0}, to_apply=%region_3.4 | reduce-window | flops 4161536 | bytes 262148 | tf_op jit(solution)/shard_map/reduce-window
  22.2 0.1 slice.16
  22.3 0.1 copy.37
  22.4 0.1 copy.38
  22.5 0.1 broadcast_add_fusion
  22.6 0.8 fusion.22
  23.4 0.1 reshape.135
  23.5 0.8 select_reduce_fusion.1
  24.4 0.1 copy.41
  24.5 0.7 mul.103
  25.2 3.1 fusion.5
  28.3 0.0 all-gather.2.cloned.1.call-done
  28.4 1.5 fusion.8
  29.9 5.1 convolution_convert_fusion.1
  35.0 282.5 %all_to_all.10 = bf16[32,48,4096]{2,1,0:T(8,128)(2,1)} all-to-all(bf16[32,48,4096]{2,1,0:T(8,128)(2,1)S(1)} %bitcast.44), channel_id=1, replica_groups=mesh['segment'=2,'expert'=16] {'segment','expert'}, dimensions={0} | all-to-all | bytes 25165824 | tf_op jit(solution)/shard_map/all_to_all | solution.py:69
  317.4 23.2 %fusion = f32[1536,1536]{1,0:T(8,128)S(1)} fusion(bf16[1536,4096]{1,0:T(8,128)(2,1)} %bitcast.46, bf16[1,4096,1536]{2,1,0:T(8,128)(2,1)} %param.20), kind=kOutput, calls=%fused_computation.2 | convolution fusion | flops 19327352832 | bytes 34603008 | tf_op jit(solution)/shard_map/dot_general | solution.py:73
  340.6 15.2 %convolution_convert_fusion = bf16[1536,4096]{1,0:T(8,128)(2,1)} fusion(bf16[1,768,4096]{2,1,0:T(8,128)(2,1)} %param.21, f32[1536,1536]{1,0:T(8,128)S(1)} %fusion), kind=kOutput, calls=%fused_computation | convolution fusion | flops 9677045760 | bytes 28311552 | tf_op jit(solution)/shard_map/dot_general | solution.py:75
  355.9 3.9 all-to-all-start.1
  359.8 0.0 copy-done.3
  359.9 0.0 copy-done.1
  359.9 0.0 copy-done.5
  359.9 0.5 fusion.16
  360.5 0.1 copy.42
  360.6 2.1 select_reduce_fusion
  362.7 277.9 %all-to-all-done.1 = bf16[32,48,4096]{2,1,0:T(8,128)(2,1)} async-done(((bf16[32,48,4096]{2,1,0:T(8,128)(2,1)}), bf16[32,48,4096]{2,1,0:T(8,128)(2,1)}, u32[]{:S(2)}, u32[]{:S(2)}) %all-to-all-start.1) | async-done | bytes 12582944 | tf_op jit(solution)/shard_map/all_to_all | solution.py:76
  640.6 6.4 convolution_add_fusion
  647.0 0.0 copy-start.4
  647.0 1.2 multiply_reduce_fusion
  648.2 0.6 fusion.27
  648.8 0.1 collective-permute-start
  648.9 1.1 collective-permute-done
  650.1 0.1 reshape.140
  650.2 0.1 constant_dynamic-slice_fusion
  650.3 0.6 copy.43
  (23 shorter events, 0.3 us)
Async XLA Ops:
  7.2 641.0 %copy-start = (bf16[1,4096,28]{1,2,0:T(8,128)(2,1)S(1)}, bf16[1,4096,28]{1,2,0:T(8,128)(2,1)}, u32[]{:S(2)}) copy-start(bf16[1,4096,28]{1,2,0:T(8,128)(2,1)} %param.15) | copy-start | bytes 688132
  7.2 21.2 %all-gather.2.cloned.1.call-start = ((), (), s32[]{:S(2)}) async-start(), calls=%async_computation.2 | async-start | bytes 1572864 | tf_op jit(solution)/shard_map/all_gather | solution.py:32
  355.9 3.9 copy-start.3
  355.9 4.0 copy-start.1
  355.9 4.0 copy-start.5
  355.9 4.5 copy-start.2
  355.9 284.7 %all-to-all-start.1 = ((bf16[32,48,4096]{2,1,0:T(8,128)(2,1)}), bf16[32,48,4096]{2,1,0:T(8,128)(2,1)}, u32[]{:S(2)}, u32[]{:S(2)}) async-start(bf16[32,48,4096]{2,1,0:T(8,128)(2,1)} %bitcast.45), calls=%async_computation.1 | async-start | bytes 25165824 | tf_op jit(solution)/shard_map/all_to_all | solution.py:76
  647.0 1.8 copy-start.4
  648.8 1.2 collective-permute-start
Sparse Core Ops, SparseCore 0:
  9.5 11.8 all-gather.1
where the time goes:
time: 659 us; the launch traced here: 658 us
  blocking collectives  282 us (43%)
  waiting for transfers between devices  280 us (42%)
  matrix products  51 us (8%)
  other arithmetic  23.5 us (4%)
  between operations  14.3 us (2%)
    all_to_all x1, blocking collectives, per_device(): lax.all_to_all(outbound, ('segment', 'expert'), split_axis=0, concat_axis...  282 us
    all_to_all x1, waiting for transfers between devices, per_device(): lax.all_to_all(result.reshape(arrived.shape), ('segment', 'expert'), spli...  278 us
    dot_general x1, matrix products, per_device(): hidden = jnp.dot(rows, expert_in[0], preferred_element_type=jnp.float32)  23.2 us
    dot_general x1, matrix products, per_device(): jnp.dot(active, expert_out[0], preferred_element_type=jnp.float32)  15.2 us
  transfers between devices with their start and end apart: 3, of which 2 were waited for; matrix products, arithmetic and copies ran while one was open for 4% of the time, Pallas kernels for 0%

commit v1 on v0

v1 whole, which is shorter than its diff:
```python
import jax
import jax.numpy as jnp
from jax import lax
from jax.sharding import PartitionSpec as P

CHUNKS = 2


def swap_cores(x):
    count = lax.axis_size("segment")
    return lax.ppermute(x, "segment", [(i, count - 1 - i) for i in range(count)])


def inverse_rms(values):
    return lax.rsqrt(jnp.mean(values * values, axis=-1, keepdims=True) + 1e-06)


def per_device(
    rollout,
    norm_gain,
    router_first,
    gain_second,
    router_second,
    expert_ids,
    copy_pick,
    later_ids,
    slot_table,
    expert_in,
    expert_out,
):
    position = lax.axis_index("segment")
    segment_count = lax.axis_size("segment")
    chip_count = lax.axis_size("expert")
    tok_rows, half = rollout.shape
    top_count = expert_ids.shape[1]
    experts_all = router_first.shape[2]
    slot_count = slot_table.shape[0]
    capacity = 3 * tok_rows * top_count // (2 * segment_count * chip_count)
    hidden_units = expert_out.shape[1]
    width = expert_out.shape[2]

    everyone = lax.all_gather(rollout, "expert", axis=0)

    expert_cols = jnp.arange(experts_all, dtype=jnp.int32)
    slot_ids = jnp.arange(slot_count, dtype=jnp.int32)
    same = slot_table[:, None] == slot_table[None, :]
    earlier = slot_ids[:, None] < slot_ids[None, :]
    copy_rank = jnp.sum((same & earlier).astype(jnp.int32), axis=0)
    slot_holders = jnp.sum(same.astype(jnp.int32), axis=0)
    here = slot_table == expert_ids[..., None]
    copies = jnp.max(jnp.where(here, slot_holders, 1), axis=-1)
    wanted = copy_pick % copies
    match = here & (copy_rank == wanted[..., None])
    hit = jnp.sum(match.astype(jnp.bfloat16), axis=1)
    order = jnp.arange(tok_rows, dtype=jnp.int32)
    before_mask = (order[None, :] < order[:, None]).astype(jnp.bfloat16)
    before = jnp.dot(before_mask, hit, preferred_element_type=jnp.float32).astype(jnp.int32)
    place = jnp.where(before < capacity, slot_ids * capacity + before, -1)
    target = jnp.sum(jnp.where(match, place[:, None, :], 0), axis=-1)
    targets = lax.all_gather(target, "expert", axis=0)

    other_half = swap_cores(rollout)
    first = position == 0
    left = jnp.where(first, rollout, other_half)
    right = jnp.where(first, other_half, rollout)
    whole = jnp.concatenate([left, right], axis=1)
    states_in = whole.astype(jnp.float32)
    normed = (states_in * inverse_rms(states_in) * norm_gain[0].astype(jnp.float32)).astype(
        jnp.bfloat16
    )
    logits = jnp.dot(normed, router_first[0], preferred_element_type=jnp.float32)
    picked = expert_ids[..., None] == expert_cols
    chosen = jnp.sum(jnp.where(picked, logits[:, None, :], 0.0), axis=-1)
    lifted = jnp.exp(chosen - jnp.max(chosen, axis=1, keepdims=True))
    gates = (lifted / jnp.sum(lifted, axis=1, keepdims=True)).astype(jnp.bfloat16)
    gates_all = lax.all_gather(gates, "expert", axis=0).astype(jnp.float32)

    chip = lax.axis_index("expert")
    own_base = (position * chip_count + chip) * capacity
    other_base = ((segment_count - 1 - position) * chip_count + chip) * capacity

    def places_in(base):
        inside = (targets >= base) & (targets < base + capacity)
        place = jnp.sum(jnp.where(inside, targets - base + 1, 0), axis=-1) - 1
        weight = jnp.sum(jnp.where(inside, gates_all, 0.0), axis=-1)
        return place, weight

    own_place, own_weight = places_in(own_base)
    other_place, other_weight = places_in(other_base)
    rows = jnp.arange(capacity, dtype=jnp.int32)

    def pick_rows(place):
        onehot = (place[:, None, :] == rows[None, :, None]).astype(jnp.bfloat16)
        got = jnp.einsum("sct,std->scd", onehot, everyone, preferred_element_type=jnp.float32)
        return got.astype(jnp.bfloat16).reshape(chip_count * capacity, half)

    other_rows = swap_cores(pick_rows(other_place))
    own_rows = pick_rows(own_place)
    left = jnp.where(first, own_rows, other_rows)
    right = jnp.where(first, other_rows, own_rows)
    full = jnp.concatenate([left, right], axis=1).astype(jnp.float32)
    scaled = full * inverse_rms(full)
    other_gain = swap_cores(norm_gain)
    inputs = jnp.concatenate(
        [
            (scaled * gain[0].astype(jnp.float32)).astype(jnp.bfloat16)
            for gain in (other_gain, norm_gain)
        ],
        axis=0,
    )
    hidden = jnp.dot(inputs, expert_in[0], preferred_element_type=jnp.float32)
    active = (jax.nn.silu(hidden[:, :hidden_units]) * hidden[:, hidden_units:]).astype(jnp.bfloat16)

    def spread(place, weight):
        return jnp.where(place[..., None] == rows, weight[..., None], 0.0).astype(jnp.bfloat16)

    weights = jnp.concatenate(
        [spread(own_place, own_weight), spread(other_place, other_weight)], axis=2
    )
    slot_rows = chip_count * capacity
    piece = width // CHUNKS
    parts = []
    for c in range(CHUNKS):
        w_out = expert_out[0, :, c * piece : (c + 1) * piece]
        result = jnp.dot(active, w_out, preferred_element_type=jnp.float32).astype(jnp.bfloat16)
        theirs = swap_cores(result[:slot_rows]).reshape(chip_count, capacity, piece)
        mine = result[slot_rows:].reshape(chip_count, capacity, piece)
        both = jnp.concatenate([mine, theirs], axis=1)
        given = jnp.einsum("stc,scd->std", weights, both, preferred_element_type=jnp.float32)
        given = given.astype(jnp.bfloat16).reshape(chip_count * tok_rows, piece)
        parts.append(lax.psum_scatter(given, "expert", scatter_dimension=0, tiled=True))
    mixed = states_in + jnp.concatenate(parts, axis=1).astype(jnp.float32)
    later = (mixed * inverse_rms(mixed) * gain_second[0].astype(jnp.float32)).astype(jnp.bfloat16)
    logp = jax.nn.log_softmax(
        jnp.dot(later, router_second[0], preferred_element_type=jnp.float32), axis=-1
    )
    later_pick = later_ids[..., None] == expert_cols
    score = jnp.sum(jnp.where(later_pick, logp[:, None, :], 0.0), axis=(1, 2))
    partner = swap_cores(score)
    ratio = jnp.where(position == 1, score - partner, partner - score)
    paired = ratio.reshape(tok_rows // 2, 2)
    column = lax.dynamic_slice_in_dim(paired, position, 1, 1)
    return (mixed.astype(jnp.bfloat16)[None], column)


def solution(mesh):
    in_specs = (
        P("expert", "segment"),
        P("segment", None),
        P("segment", None, None),
        P("segment", None),
        P("segment", None, None),
        P("expert", None),
        P("expert", None),
        P("expert", None),
        P(),
        P(("segment", "expert"), None, None),
        P(("segment", "expert"), None, None),
    )
    out_specs = (P("segment", "expert", None), P("expert", "segment"))
    return jax.shard_map(
        per_device, mesh=mesh, in_specs=in_specs, out_specs=out_specs, check_vma=False
    )
```

time: 659 us -> 612 us (0.929)
  blocking collectives: 282 us -> 82 us
  waiting for transfers between devices: 280 us -> 424 us
  matrix products: 51 us -> 63.3 us
    reduce_scatter x0 -> x2, waiting for transfers between devices: none -> 336 us  [per_device(): lax.psum_scatter(given, 'expert', scatter_dimension=0, tiled=True)]
    all_to_all x1 -> x0, blocking collectives: 282 us -> none  [per_device(): lax.all_to_all(outbound, ('segment', 'expert'), split_axis=0, concat_axis...]
    all_to_all x1 -> x0, waiting for transfers between devices: 278 us -> none  [per_device(): lax.all_to_all(result.reshape(arrived.shape), ('segment', 'expert'), spli...]
    all_gather x0 -> x2, blocking collectives: none -> 82 us  [the longest x1 43.8 us: per_device(): targets = lax.all_gather(target, 'expert', axis=0)]
    all_gather x1, waiting for transfers between devices: 0.02 us -> 70.1 us  [per_device(): everyone = lax.all_gather(rollout, 'expert', axis=0)]
    ppermute x1 -> x6, waiting for transfers between devices: 1.14 us -> 17 us  [swap_cores(): lax.ppermute(x, 'segment', [(i, count - 1 - i) for i in range(count)])]
    dot_general x4 -> x8, matrix products: 49.9 us -> 61 us  [the longest x1 24.3 us: per_device(): hidden = jnp.dot(inputs, expert_in[0], preferred_element_type=jnp.float32)]
    another operation x3 -> x0, other arithmetic: 9.15 us -> none
  transfers between devices with their start and end apart: 3 -> 9, of which waited for: 2 -> 6; matrix products, arithmetic and copies ran while one was open for 4% -> 4% of each run, Pallas kernels for 0% -> 0%
where the time goes in v1:
time: 612 us; the launch traced here: 609 us
  waiting for transfers between devices  424 us (69%)
  blocking collectives  82 us (13%)
  matrix products  63.3 us (10%)
  other arithmetic  18.2 us (3%)
  between operations  14.1 us (2%)
  local copies, waits for them, and re-layouts  7 us (1%)
    reduce_scatter x2, waiting for transfers between devices, per_device(): lax.psum_scatter(given, 'expert', scatter_dimension=0, tiled=True)  336 us
    all_gather x1, waiting for transfers between devices, per_device(): everyone = lax.all_gather(rollout, 'expert', axis=0)  70.1 us
    all_gather x1, blocking collectives, per_device(): targets = lax.all_gather(target, 'expert', axis=0)  43.8 us
    all_gather x1, blocking collectives, per_device(): gates_all = lax.all_gather(gates, 'expert', axis=0).astype(jnp.float32)  38.2 us
    dot_general x1, matrix products, per_device(): hidden = jnp.dot(inputs, expert_in[0], preferred_element_type=jnp.float32)  24.3 us
    ppermute x6, waiting for transfers between devices, swap_cores(): lax.ppermute(x, 'segment', [(i, count - 1 - i) for i in range(count)])  17 us
    dot_general x2, matrix products, per_device(): jnp.dot(active, w_out, preferred_element_type=jnp.float32)  15.3 us
  transfers between devices with their start and end apart: 9, of which 6 were waited for; matrix products, arithmetic and copies ran while one was open for 4% of the time, Pallas kernels for 0%

profile of v1, /device:TPU:0, one launch (start us, length us, event | category | flops | bytes accessed | tf_op | source)
XLA Modules:
  0.0 609.4 jit_solution(10013019264550102192)
XLA Ops:
  7.2 0.7 all-gather.4.cloned.1.call-update
  8.0 0.8 convert_reduce_fusion
  8.8 0.8 fusion.41
  9.6 0.8 add_select_fusion.1
  10.4 0.8 fusion.45
  11.2 0.1 add_select_fusion
  11.3 0.8 select_reduce_fusion
  12.2 43.8 %all-gather = s32[2048,8]{0,1:T(8,128)S(1)} all-gather(s32[128,8]{0,1:T(8,128)S(1)} %select_reduce_fusion), channel_id=2, replica_groups=mesh['segment'=2,'expert'=16] {'expert'}, dimensions={0}, use_global_device_ids=true | all-gather | bytes 69632 | tf_op jit(solution)/shard_map/all_gather | solution.py:60
  55.9 0.1 fusion.47
  56.0 70.1 %all-gather.4.cloned.1.call-done = bf16[2048,2048]{1,0:T(8,128)(2,1)} async-done(((bf16[128,2048]{1,0:T(8,128)(2,1)}), bf16[2048,2048]{1,0:T(8,128)(2,1)}) %all-gather.4.cloned.1.call-update) | async-done | bytes 8388624 | tf_op jit(solution)/shard_map/all_gather | solution.py:42
  126.1 4.6 convolution_convert_fusion.2
  130.8 0.1 collective-permute-start.1
  130.8 0.5 collective-permute-start.2
  131.4 5.2 collective-permute-done.2
  136.6 4.6 convolution_convert_fusion.3
  141.3 2.3 bitcast_select_fusion.1
  143.6 1.7 fusion.4
  145.3 4.9 fusion.2
  150.2 24.3 %fusion.5 = f32[1536,1536]{1,0:T(8,128)S(1)} fusion(bf16[768,4096]{1,0:T(8,128)(2,1)} %get-tuple-element.19, bf16[768,4096]{1,0:T(8,128)(2,1)S(1)} %get-tuple-element.18, bf16[1,4096,1536]{2,1,0:T(8,128)(2,1)} %param.20), kind=kOutput, calls=%fused_computation.7 | convolution fusion | flops 19352518656 | bytes 34603008 | tf_op jit(solution)/shard_map/dot_general | solution.py:111
  174.4 1.5 fusion.24
  176.0 8.0 %convolution_convert_fusion.1 = bf16[1536,2048]{1,0:T(8,128)(2,1)S(1)} fusion(bf16[1536,768]{1,0:T(8,128)(2,1)S(1)} %fusion.24, bf16[1,768,4096]{2,1,0:T(8,128)(2,1)} %param.21), kind=kOutput, calls=%fused_computation.13 | convolution fusion | flops 4834983936 | bytes 11796480 | tf_op jit(solution)/shard_map/dot_general | solution.py:125
  184.0 2.5 fusion.56
  186.5 0.1 collective-permute-start.3
  186.7 0.4 collective-permute-start
  187.1 6.1 %collective-permute-done = bf16[128,2048]{1,0:T(8,128)(2,1)S(1)} collective-permute-done((bf16[128,2048]{1,0:T(8,128)(2,1)S(1)}, bf16[128,2048]{1,0:T(8,128)(2,1)S(1)}, u32[]{:S(2)}, u32[]{:S(2)}) %collective-permute-start) | collective-permute-done | bytes 524320 | tf_op jit(solution)/shard_map/ppermute | solution.py:11
  193.2 0.1 broadcast_select_fusion.1
  193.3 0.3 fusion.29
  193.6 0.5 copy-done.1
  194.0 0.5 fusion.32
  194.7 38.2 %all_gather.18 = bf16[16,128,8]{1,2,0:T(8,128)(2,1)S(1)} all-gather(bf16[1,128,8]{1,2,0:T(8,128)(2,1)S(1)} %fusion.51), channel_id=1, replica_groups=mesh['segment'=2,'expert'=16] {'expert'}, dimensions={0}, use_global_device_ids=true | all-gather | bytes 34816 | tf_op jit(solution)/shard_map/all_gather | solution.py:76
  232.9 0.1 fusion.43
  233.1 7.6 %fusion.21 = bf16[16,128,2048]{2,1,0:T(8,128)(2,1)} fusion(bf16[16,48,2048]{2,1,0:T(8,128)(2,1)} %bitcast.16, bf16[16,48,2048]{2,1,0:T(8,128)(2,1)S(1)} %bitcast.66, bf16[16,128,48]{1,2,0:T(8,128)(2,1)S(1)} %select_convert_fusion, bf16[16,128,48]{1,2,0:T(8,128)(2,1)S(1)} %select_convert_fusion.1), kind=kOutput, calls=%fused_computation.24 | convolution fusion | flops 822870016 | bytes 15073280 | tf_op jit(solution)/shard_map/stc,scd->std/dot_general | solution.py:129
  240.7 1.6 copy-done.6
  242.3 7.3 %convolution_convert_fusion = bf16[1536,2048]{1,0:T(8,128)(2,1)S(1)} fusion(bf16[1536,768]{1,0:T(8,128)(2,1)S(1)} %copy-done.6, bf16[1,768,4096]{2,1,0:T(8,128)(2,1)} %param.21), kind=kOutput, calls=%fused_computation.12 | convolution fusion | flops 4834983936 | bytes 11796480 | tf_op jit(solution)/shard_map/dot_general | solution.py:125
  249.6 0.8 fusion.57
  250.4 0.1 collective-permute-start.4
  250.5 5.6 collective-permute-done.4
  256.2 4.5 fusion.18
  260.8 0.7 copy-done.16
  261.5 153.1 %reduce-scatter.3.cloned.1.call-done = bf16[128,2048]{1,0:T(8,128)(2,1)} async-done(((bf16[2048,2048]{1,0:T(8,128)(2,1)}), bf16[128,2048]{1,0:T(8,128)(2,1)}) %reduce-scatter.3.cloned.1.call-update) | async-done | bytes 524304 | tf_op jit(solution)/shard_map/reduce_scatter | solution.py:131
  414.5 182.6 %reduce-scatter.5.cloned.1.call-done = bf16[128,2048]{1,0:T(8,128)(2,1)} async-done(((bf16[2048,2048]{1,0:T(8,128)(2,1)}), bf16[128,2048]{1,0:T(8,128)(2,1)}) %reduce-scatter.5.cloned.1.call-update) | async-done | bytes 524304 | tf_op jit(solution)/shard_map/reduce_scatter | solution.py:131
  597.2 1.7 multiply_reduce_fusion
  598.9 1.8 fusion.58
  600.7 0.1 collective-permute-start.5
  600.8 1.2 add_convert_fusion
  602.1 0.1 reshape.212
  602.2 0.1 constant_dynamic-slice_fusion
  602.3 0.6 copy.45
  (63 shorter events, 0.6 us)
Async XLA Ops:
  7.2 591.7 %copy-start = (bf16[1,4096,28]{1,2,0:T(8,128)(2,1)S(1)}, bf16[1,4096,28]{1,2,0:T(8,128)(2,1)}, u32[]{:S(2)}) copy-start(bf16[1,4096,28]{1,2,0:T(8,128)(2,1)} %param.15) | copy-start | bytes 688132
  7.2 118.9 %all-gather.4.cloned.1.call-start = ((), (), s32[]{:S(2)}) async-start(), calls=%async_computation.4 | async-start | bytes 8912896 | tf_op jit(solution)/shard_map/all_gather | solution.py:42
  7.9 406.6 %reduce-scatter.3.cloned.1.call-start = ((), (), s32[]{:S(2)}) async-start(), calls=%async_computation.2 | async-start | bytes 8912896 | tf_op jit(solution)/shard_map/reduce_scatter | solution.py:131
  126.1 4.7 copy-start.15
  130.8 10.5 %collective-permute-start.1 = (bf16[768,2048]{1,0:T(8,128)(2,1)S(1)}, bf16[768,2048]{1,0:T(8,128)(2,1)}, u32[]{:S(2)}, u32[]{:S(2)}) collective-permute-start(bf16[768,2048]{1,0:T(8,128)(2,1)S(1)} %bitcast.68), channel_id=1, source_target_pairs={{0,16},{16,0},{1,17},{17,1},{2,18},{18,2},{3,19},{19,3},{4,20},{20... | collective-permute-start | bytes 9437192 | tf_op jit(solution)/shard_map/ppermute | solution.py:11
  130.8 5.8 collective-permute-start.2
  176.0 8.0 %copy-start.5 = (bf16[1536,768]{1,0:T(8,128)(2,1)}, bf16[1536,768]{1,0:T(8,128)(2,1)S(1)}, u32[]{:S(2)}) copy-start(bf16[1536,768]{1,0:T(8,128)(2,1)S(1)} %fusion.24) | copy-start | bytes 7077892
  184.0 2.7 copy-start.7
  184.0 10.0 %copy-start.18 = (bf16[1,4096,28]{1,2,0:T(8,128)(2,1)S(1)}, bf16[1,4096,28]{1,2,0:T(8,128)(2,1)}, u32[]{:S(2)}) copy-start(bf16[1,4096,28]{1,2,0:T(8,128)(2,1)} %param.13) | copy-start | bytes 688132
  186.5 8.0 %copy-start.14 = (s32[128,8]{0,1:T(8,128)S(1)}, s32[128,8]{0,1:T(8,128)}, u32[]{:S(2)}) copy-start(s32[128,8]{0,1:T(8,128)} %param.16) | copy-start | bytes 12292
  186.5 46.5 %collective-permute-start.3 = (bf16[768,2048]{1,0:T(8,128)(2,1)}, bf16[768,2048]{1,0:T(8,128)(2,1)}, u32[]{:S(2)}, u32[]{:S(2)}) collective-permute-start(bf16[768,2048]{1,0:T(8,128)(2,1)} %get-tuple-element.21), channel_id=1, source_target_pairs={{0,16},{16,0},{1,17},{17,1},{2,18},{18,2},{3,19},{19,3},{4,20},{20... | collective-permute-start | bytes 9437192 | tf_op jit(solution)/shard_map/ppermute | solution.py:11
  186.7 6.5 %collective-permute-start = (bf16[128,2048]{1,0:T(8,128)(2,1)S(1)}, bf16[128,2048]{1,0:T(8,128)(2,1)S(1)}, u32[]{:S(2)}, u32[]{:S(2)}) collective-permute-start(bf16[128,2048]{1,0:T(8,128)(2,1)S(1)} %copy-done.7), channel_id=1, source_target_pairs={{0,16},{16,0},{1,17},{17,1},{2,18},{18,2},{3,19},{19,3},{4,20},{20... | collective-permute-start | bytes 1572872 | tf_op jit(solution)/shard_map/ppermute | solution.py:11
  193.2 0.8 copy-start.1
  193.3 1.3 copy-start.3
  233.0 7.6 %copy-start.10 = (bf16[16,128,48]{1,2,0:T(8,128)(2,1)}, bf16[16,128,48]{1,2,0:T(8,128)(2,1)S(1)}, u32[]{:S(2)}) copy-start(bf16[16,128,48]{1,2,0:T(8,128)(2,1)S(1)} %select_convert_fusion) | copy-start | bytes 589828
  233.0 7.6 %copy-start.12 = (bf16[16,128,48]{1,2,0:T(8,128)(2,1)}, bf16[16,128,48]{1,2,0:T(8,128)(2,1)S(1)}, u32[]{:S(2)}) copy-start(bf16[16,128,48]{1,2,0:T(8,128)(2,1)S(1)} %select_convert_fusion.1) | copy-start | bytes 589828
  240.6 1.7 copy-start.6
  240.7 356.5 %reduce-scatter.5.cloned.1.call-start = ((), (), s32[]{:S(2)}) async-start(), calls=%async_computation.3 | async-start | bytes 8912896 | tf_op jit(solution)/shard_map/reduce_scatter | solution.py:131
  249.6 6.6 %copy-start.11 = (bf16[16,128,48]{1,2,0:T(8,128)(2,1)S(1)}, bf16[16,128,48]{1,2,0:T(8,128)(2,1)}, u32[]{:S(2)}) copy-start(bf16[16,128,48]{1,2,0:T(8,128)(2,1)} %copy-done.10) | copy-start | bytes 589828
  249.6 6.6 %copy-start.13 = (bf16[16,128,48]{1,2,0:T(8,128)(2,1)S(1)}, bf16[16,128,48]{1,2,0:T(8,128)(2,1)}, u32[]{:S(2)}) copy-start(bf16[16,128,48]{1,2,0:T(8,128)(2,1)} %copy-done.12) | copy-start | bytes 589828
  250.4 5.7 collective-permute-start.4
  260.7 0.7 copy-start.16
  260.7 336.4 %copy-start.2 = (bf16[128,2048]{1,0:T(8,128)(2,1)S(1)}, bf16[128,2048]{1,0:T(8,128)(2,1)}, u32[]{:S(2)}) copy-start(bf16[128,2048]{1,0:T(8,128)(2,1)} %copy-done.1) | copy-start | bytes 1572868
  260.7 336.4 %copy-start.4 = (bf16[128,2048]{1,0:T(8,128)(2,1)S(1)}, bf16[128,2048]{1,0:T(8,128)(2,1)}, u32[]{:S(2)}) copy-start(bf16[128,2048]{1,0:T(8,128)(2,1)} %copy-done.3) | copy-start | bytes 1572868
  260.8 339.9 %copy-start.17 = (s32[128,8]{0,1:T(8,128)S(1)}, s32[128,8]{0,1:T(8,128)}, u32[]{:S(2)}) copy-start(s32[128,8]{0,1:T(8,128)} %param.18) | copy-start | bytes 12292
  414.5 186.3 %copy-start.8 = (bf16[128,2048]{1,0:T(8,128)(2,1)S(1)}, bf16[128,2048]{1,0:T(8,128)(2,1)}, u32[]{:S(2)}) copy-start(bf16[128,2048]{1,0:T(8,128)(2,1)} %reduce-scatter.3.cloned.1.call-done) | copy-start | bytes 1572868
  597.2 3.7 copy-start.9
  600.7 1.3 collective-permute-start.5
Sparse Core Ops, SparseCore 0:
  10.8 115.3 all-gather.3
  240.8 173.7 reduce-scatter.2
  416.8 180.2 reduce-scatter.4

commit v2 on v1

--- a/solution.py
+++ b/solution.py
@@ -1,9 +1,240 @@
+import functools
+import math
+
 import jax
 import jax.numpy as jnp
 from jax import lax
+from jax.experimental import pallas as pl
+from jax.experimental.pallas import tpu as pltpu
 from jax.sharding import PartitionSpec as P
 
-CHUNKS = 2
+LANES = 128
+VMEM_BUDGET = 24 << 20
+MESH = pl.DeviceIdType.MESH
+
+
+def grid_sides(count):
+    outer = 1
+    while outer**3 < count:
+        outer *= 2
+    rest = count // outer
+    middle = 1
+    while middle**2 < rest:
+        middle *= 2
+    return outer, middle, rest // middle
+
+
+def return_kernel(sides, chunks, act, w_out, wts, out, mine, give, got, *rest):
+    n_a, n_b, n_c = sides
+    bufs, sems = rest[:12], rest[12:]
+    seg = lax.axis_index("segment")
+    me = lax.axis_index("expert")
+    a, b, c = me // (n_b * n_c), (me // n_c) % n_b, me % n_c
+    blocks = n_a * n_b * n_c
+    slot_rows = mine.shape[1]
+    cap = slot_rows // blocks
+    wide = mine.shape[2]
+    half = wide // 2
+    tile = math.gcd(slot_rows, 256)
+
+    def at(na, nb, nc):
+        return (seg, (na * n_b + nb) * n_c + nc)
+
+    partner = (1 - seg, me)
+
+    def peer_a(k):
+        return at((a + k) % n_a, b, c)
+
+    def peer_b(k):
+        return at(a, (b + k) % n_b, c)
+
+    def peer_c(k):
+        return at(a, b, (c + k) % n_c)
+
+    barrier = pltpu.get_barrier_semaphore()
+    friends = [partner]
+    friends += [peer_a(k) for k in range(1, n_a)]
+    friends += [peer_b(k) for k in range(1, n_b)]
+    friends += [peer_c(k) for k in range(1, n_c)]
+    for friend in friends:
+        pl.semaphore_signal(barrier, inc=1, device_id=friend, device_id_type=MESH)
+    pl.semaphore_wait(barrier, len(friends))
+
+    orders = (
+        ((c, n_c, peer_c), (b, n_b, peer_b)),
+        ((b, n_b, peer_b), (c, n_c, peer_c)),
+    )
+
+    def swap(j):
+        return pltpu.make_async_remote_copy(
+            src_ref=give.at[j % 2],
+            dst_ref=got.at[j],
+            send_sem=sems[0].at[j % 2],
+            recv_sem=sems[1].at[j],
+            device_id=partner,
+            device_id_type=MESH,
+        )
+
+    def sends(half_index, phase, j):
+        first, second = orders[half_index]
+        src, dst = bufs[half_index * 6 + phase * 2 : half_index * 6 + phase * 2 + 2]
+        send, recv = sems[2 + half_index * 6 + phase * 2 : 4 + half_index * 6 + phase * 2]
+        place, side, peer = (first, second, (a, n_a, peer_a))[phase]
+        return [
+            pltpu.make_async_remote_copy(
+                src_ref=src.at[j % 2, (place + k) % side],
+                dst_ref=dst.at[j, k - 1],
+                send_sem=send.at[j % 2, k - 1],
+                recv_sem=recv.at[j, k - 1],
+                device_id=peer(k),
+                device_id_type=MESH,
+            )
+            for k in range(1, side)
+        ]
+
+    def project(j):
+        columns = pl.ds(pl.multiple_of(j * wide, wide), wide)
+
+        def one(r, dest, base):
+            rows = pl.ds(pl.multiple_of(r * tile, tile), tile)
+            source = pl.ds(pl.multiple_of(base + r * tile, tile), tile)
+            dest[j % 2, rows, :] = jnp.dot(
+                act[source, :], w_out[:, columns], preferred_element_type=jnp.float32
+            ).astype(jnp.bfloat16)
+
+        @pl.loop(0, slot_rows // tile)
+        def _(r):
+            one(r, give, 0)
+
+        swap(j).start()
+
+        @pl.loop(0, slot_rows // tile)
+        def _(r):
+            one(r, mine, slot_rows)
+
+    def spread(j):
+        swap(j).wait()
+
+        @pl.loop(0, blocks)
+        def _(d):
+            da, db, dc = d // (n_b * n_c), (d // n_c) % n_b, d % n_c
+            rows = pl.ds(pl.multiple_of(d * cap, cap), cap)
+            both = jnp.concatenate([mine[j % 2, rows, :], got[j, rows, :]], axis=0)
+            part = jnp.dot(wts[d], both, preferred_element_type=jnp.float32)
+            part = part.astype(jnp.bfloat16)
+            bufs[0][j % 2, dc, db * n_a + da] = part[:, :half]
+            bufs[6][j % 2, db, dc * n_a + da] = part[:, half:]
+
+        for half_index in range(2):
+            for copy in sends(half_index, 0, j):
+                copy.start()
+
+    def first_sum(j):
+        for half_index in range(2):
+            (place, side, _), (_, side2, _) = orders[half_index]
+            src, dst, nxt = bufs[half_index * 6 : half_index * 6 + 3]
+            for copy in sends(half_index, 0, j):
+                copy.wait()
+
+            @pl.loop(0, side2 * n_a)
+            def _(d):
+                total = src[j % 2, place, d].astype(jnp.float32)
+                for k in range(side - 1):
+                    total += dst[j, k, d].astype(jnp.float32)
+                nxt[j % 2, d // n_a, d % n_a] = total.astype(jnp.bfloat16)
+
+            for copy in sends(half_index, 1, j):
+                copy.start()
+
+    def second_sum(j):
+        for half_index in range(2):
+            place, side, _ = orders[half_index][1]
+            src, dst, nxt = bufs[half_index * 6 + 2 : half_index * 6 + 5]
+            for copy in sends(half_index, 1, j):
+                copy.wait()
+
+            @pl.loop(0, n_a)
+            def _(d):
+                total = src[j % 2, place, d].astype(jnp.float32)
+                for k in range(side - 1):
+                    total += dst[j, k, d].astype(jnp.float32)
+                nxt[j % 2, d] = total.astype(jnp.bfloat16)
+
+            for copy in sends(half_index, 2, j):
+                copy.start()
+
+    def last_sum(j):
+        for half_index in range(2):
+            src, dst = bufs[half_index * 6 + 4 : half_index * 6 + 6]
+            for copy in sends(half_index, 2, j):
+                copy.wait()
+            total = src[j % 2, a].astype(jnp.float32)
+            for k in range(n_a - 1):
+                total += dst[j, k].astype(jnp.float32)
+            columns = pl.ds(pl.multiple_of(j * wide + half_index * half, half), half)
+            out[:, columns] = total
+
+    stages = (project, spread, first_sum, second_sum, last_sum)
+
+    @pl.loop(0, chunks + len(stages) - 1)
+    def _(step):
+        for lag, stage in enumerate(stages):
+
+            @pl.when((step >= lag) & (step - lag < chunks))
+            def _():
+                stage(step - lag)
+
+
+def return_call(sides, act, w_out, wts):
+    n_a, n_b, n_c = sides
+    tok_rows = wts.shape[1]
+    slot_rows = act.shape[0] // 2
+    half, wide = LANES, 2 * LANES
+    block_bytes = tok_rows * half * 2
+    chunk_bytes = slot_rows * wide * 2
+    for first, second in ((n_c, n_b), (n_b, n_c)):
+        chunk_bytes += block_bytes * n_a * (second * (first - 1) + second - 1)
+        chunk_bytes += block_bytes * (n_a - 1)
+    chunks = w_out.shape[1] // wide
+    while chunks % 2 == 0 and chunks * chunk_bytes > VMEM_BUDGET:
+        chunks //= 2
+
+    def bf(*shape):
+        return pltpu.VMEM(shape, jnp.bfloat16)
+
+    def dma(*shape):
+        return pltpu.SemaphoreType.DMA(shape)
+
+    scratch = [bf(2, slot_rows, wide), bf(2, slot_rows, wide), bf(chunks, slot_rows, wide)]
+    sems = [dma(2), dma(chunks)]
+    for first, second in ((n_c, n_b), (n_b, n_c)):
+        scratch += [
+            bf(2, first, second * n_a, tok_rows, half),
+            bf(chunks, first - 1, second * n_a, tok_rows, half),
+            bf(2, second, n_a, tok_rows, half),
+            bf(chunks, second - 1, n_a, tok_rows, half),
+            bf(2, n_a, tok_rows, half),
+            bf(chunks, n_a - 1, tok_rows, half),
+        ]
+        for side in (first, second, n_a):
+            sems += [dma(2, side - 1), dma(chunks, side - 1)]
+    piece = chunks * wide
+    call = pl.pallas_call(
+        functools.partial(return_kernel, sides, chunks),
+        out_shape=jax.ShapeDtypeStruct((tok_rows, piece), jnp.float32),
+        in_specs=[pl.BlockSpec(memory_space=pltpu.VMEM)] * 3,
+        out_specs=pl.BlockSpec(memory_space=pltpu.VMEM),
+        scratch_shapes=scratch + sems,
+        compiler_params=pltpu.CompilerParams(
+            collective_id=0, has_side_effects=True, vmem_limit_bytes=60 * 1024 * 1024
+        ),
+        name="return_sum",
+    )
+    parts = [
+        call(act, w_out[:, start : start + piece], wts)
+        for start in range(0, w_out.shape[1], piece)
+    ]
+    return parts[0] if len(parts) == 1 else jnp.concatenate(parts, axis=1)
 
 
 def swap_cores(x):
@@ -37,7 +268,6 @@
     slot_count = slot_table.shape[0]
     capacity = 3 * tok_rows * top_count // (2 * segment_count * chip_count)
     hidden_units = expert_out.shape[1]
-    width = expert_out.shape[2]
 
     everyone = lax.all_gather(rollout, "expert", axis=0)
 
@@ -57,8 +287,6 @@
     before = jnp.dot(before_mask, hit, preferred_element_type=jnp.float32).astype(jnp.int32)
     place = jnp.where(before < capacity, slot_ids * capacity + before, -1)
     target = jnp.sum(jnp.where(match, place[:, None, :], 0), axis=-1)
-    targets = lax.all_gather(target, "expert", axis=0)
-
     other_half = swap_cores(rollout)
     first = position == 0
     left = jnp.where(first, rollout, other_half)
@@ -73,7 +301,10 @@
     chosen = jnp.sum(jnp.where(picked, logits[:, None, :], 0.0), axis=-1)
     lifted = jnp.exp(chosen - jnp.max(chosen, axis=1, keepdims=True))
     gates = (lifted / jnp.sum(lifted, axis=1, keepdims=True)).astype(jnp.bfloat16)
-    gates_all = lax.all_gather(gates, "expert", axis=0).astype(jnp.float32)
+    packed = jnp.concatenate([target.astype(jnp.float32), gates.astype(jnp.float32)], axis=1)
+    packed = lax.all_gather(packed, "expert", axis=0)
+    targets = packed[..., :top_count].astype(jnp.int32)
+    gates_all = packed[..., top_count:]
 
     chip = lax.axis_index("expert")
     own_base = (position * chip_count + chip) * capacity
@@ -87,12 +318,13 @@
 
     own_place, own_weight = places_in(own_base)
     other_place, other_weight = places_in(other_base)
-    rows = jnp.arange(capacity, dtype=jnp.int32)
+    room = -(-capacity // 16) * 16
+    rows = jnp.arange(room, dtype=jnp.int32)
 
     def pick_rows(place):
         onehot = (place[:, None, :] == rows[None, :, None]).astype(jnp.bfloat16)
         got = jnp.einsum("sct,std->scd", onehot, everyone, preferred_element_type=jnp.float32)
-        return got.astype(jnp.bfloat16).reshape(chip_count * capacity, half)
+        return got.astype(jnp.bfloat16).reshape(chip_count * room, half)
 
     other_rows = swap_cores(pick_rows(other_place))
     own_rows = pick_rows(own_place)
@@ -117,19 +349,8 @@
     weights = jnp.concatenate(
         [spread(own_place, own_weight), spread(other_place, other_weight)], axis=2
     )
-    slot_rows = chip_count * capacity
-    piece = width // CHUNKS
-    parts = []
-    for c in range(CHUNKS):
-        w_out = expert_out[0, :, c * piece : (c + 1) * piece]
-        result = jnp.dot(active, w_out, preferred_element_type=jnp.float32).astype(jnp.bfloat16)
-        theirs = swap_cores(result[:slot_rows]).reshape(chip_count, capacity, piece)
-        mine = result[slot_rows:].reshape(chip_count, capacity, piece)
-        both = jnp.concatenate([mine, theirs], axis=1)
-        given = jnp.einsum("stc,scd->std", weights, both, preferred_element_type=jnp.float32)
-        given = given.astype(jnp.bfloat16).reshape(chip_count * tok_rows, piece)
-        parts.append(lax.psum_scatter(given, "expert", scatter_dimension=0, tiled=True))
-    mixed = states_in + jnp.concatenate(parts, axis=1).astype(jnp.float32)
+    summed = return_call(grid_sides(chip_count), active, expert_out[0], weights)
+    mixed = states_in + summed
     later = (mixed * inverse_rms(mixed) * gain_second[0].astype(jnp.float32)).astype(jnp.bfloat16)
     logp = jax.nn.log_softmax(
         jnp.dot(later, router_second[0], preferred_element_type=jnp.float32), axis=-1

time: 612 us -> 350 us (0.57)
  waiting for transfers between devices: 424 us -> 72.9 us
  Pallas kernels: 0 us -> 161 us
  blocking collectives: 82 us -> 44.3 us
  matrix products: 63.3 us -> 34 us
  local copies, waits for them, and re-layouts: 7 us -> 0.87 us
    reduce_scatter x2 -> x0, waiting for transfers between devices: 336 us -> none  [per_device(): lax.psum_scatter(given, 'expert', scatter_dimension=0, tiled=True)]
    pallas_call x0 -> x1, Pallas kernels: none -> 161 us  [return_call(): call(act, w_out[:, start:start + piece], wts)]
    all_gather x2 -> x1, blocking collectives: 82 us -> 44.3 us  [per_device(): packed = lax.all_gather(packed, 'expert', axis=0)]
    dot_general x4 -> x0, matrix products: 27.4 us -> none  [the longest x2 15.3 us: per_device(): jnp.dot(active, w_out, preferred_element_type=jnp.float32)]
    ppermute x6 -> x4, waiting for transfers between devices: 17 us -> 6.3 us  [swap_cores(): lax.ppermute(x, 'segment', [(i, count - 1 - i) for i in range(count)])]
  transfers between devices with their start and end apart: 9 -> 5, of which waited for: 6 -> 3; matrix products, arithmetic and copies ran while one was open for 4% -> 3% of each run, Pallas kernels for 0% -> 0%
where the time goes in v2:
time: 350 us
  Pallas kernels  161 us (46%)
  waiting for transfers between devices  72.9 us (21%)
  blocking collectives  44.3 us (13%)
  matrix products  34 us (10%)
  other arithmetic  21.7 us (6%)
  between operations  14.3 us (4%)
    pallas_call x1, Pallas kernels, return_call(): call(act, w_out[:, start:start + piece], wts)  161 us
    all_gather x1, waiting for transfers between devices, per_device(): everyone = lax.all_gather(rollout, 'expert', axis=0)  65.9 us
    all_gather x1, blocking collectives, per_device(): packed = lax.all_gather(packed, 'expert', axis=0)  44.3 us
    dot_general x1, matrix products, per_device(): hidden = jnp.dot(inputs, expert_in[0], preferred_element_type=jnp.float32)  24.3 us
  transfers between devices with their start and end apart: 5, of which 3 were waited for; matrix products, arithmetic and copies ran while one was open for 3% of the time, Pallas kernels for 0%

profile of v2, /device:TPU:0, one launch (start us, length us, event | category | flops | bytes accessed | tf_op | source)
XLA Modules:
  0.0 349.8 jit_solution(2017052542637756679)
XLA Ops:
  7.2 0.0 copy-start
  7.2 0.0 copy-start.1
  7.2 0.0 all-gather.4.cloned.1.call-start
  7.2 0.7 all-gather.4.cloned.1.call-update
  7.9 0.6 collective-permute-start
  8.5 0.7 mul.140
  9.2 0.8 convert_reduce_fusion
  10.0 0.8 fusion.25
  10.8 0.8 add_select_fusion.1
  11.7 0.8 fusion.27
  12.4 0.1 add_select_fusion
  12.6 0.8 select_reduce_fusion
  13.4 0.0 collective-permute-done
  13.4 1.1 broadcast_select_fusion.1
  14.6 0.3 fusion.11
  14.9 1.5 fusion.15
  16.4 0.0 copy-done.1
  16.4 0.1 select_reduce_fusion.2
  16.5 44.3 %all-gather = f32[2048,16]{0,1:T(8,128)S(1)} all-gather(f32[128,16]{0,1:T(8,128)S(1)} %pad_maximum_fusion.3), channel_id=2, replica_groups=mesh['segment'=2,'expert'=16] {'expert'}, dimensions={0}, use_global_device_ids=true | all-gather | bytes 139264 | tf_op jit(solution)/shard_map/all_gather | solution.py:305
  60.9 65.9 %all-gather.4.cloned.1.call-done = bf16[2048,2048]{1,0:T(8,128)(2,1)} async-done(((bf16[128,2048]{1,0:T(8,128)(2,1)}), bf16[2048,2048]{1,0:T(8,128)(2,1)}) %all-gather.4.cloned.1.call-update) | async-done | bytes 8388624 | tf_op jit(solution)/shard_map/all_gather | solution.py:272
  126.8 4.8 %convolution_convert_fusion = bf16[16,48,2048]{2,1,0:T(8,128)(2,1)S(1)} fusion(bf16[16,128,2048]{2,1,0:T(8,128)(2,1)} %bitcast.29, s32[16,128]{1,0:T(8,128)S(1)} %broadcast_add_fusion), kind=kOutput, calls=%fused_computation.15 | convolution fusion | flops 404324352 | bytes 11542528 | tf_op jit(solution)/shard_map/sct,std->scd/dot_general | solution.py:326
  131.5 0.1 collective-permute-start.1
  131.6 0.0 copy-done.3
  131.6 0.5 collective-permute-start.2
  132.1 0.0 copy-done.2
  132.1 5.1 %collective-permute-done.2 = bf16[1,4096]{1,0:T(2,128)(2,1)S(1)} collective-permute-done((bf16[1,4096]{1,0:T(2,128)(2,1)S(1)}, bf16[1,4096]{1,0:T(2,128)(2,1)S(1)}, u32[]{:S(2)}, u32[]{:S(2)}) %collective-permute-start.2) | collective-permute-done | bytes 8224 | tf_op jit(solution)/shard_map/ppermute | solution.py:242
  137.3 1.6 select_convert_fusion
  138.9 1.1 pad_maximum_fusion.2.wts
  140.0 0.0 slice-done
  140.0 0.0 slice-done.1
  140.0 1.2 convolution_convert_fusion.1
  141.3 0.0 collective-permute-done.1
  141.3 0.6 bitcast_select_fusion.1
  141.9 1.5 fusion.4
  143.4 4.9 %fusion.2 = (bf16[768,4096]{1,0:T(8,128)(2,1)S(1)}, bf16[768,4096]{1,0:T(8,128)(2,1)}) fusion(f32[4096]{0:T(1024)S(1)} %bitcast.40, f32[768]{0:T(1024)S(1)} %add_rsqrt_fusion, bf16[768,2048]{1,0:T(8,128)(2,1)S(1)} %get-tuple-element.21, bf16[768,2048]{1,0:T(8,128)(2,1)S(1)} %get-tuple-element.20, f32[4096]{0:T(1024)S(1)} %bitcast.39), kind=kLoop, calls=%fused_computation.4 | loop fusion | flops 28311552 | bytes 18910208 | tf_op jit(solution)/shard_map/convert_element_type | solution.py:338
  148.3 24.3 %fusion.5 = f32[1536,1536]{1,0:T(8,128)S(1)} fusion(bf16[768,4096]{1,0:T(8,128)(2,1)} %get-tuple-element.19, bf16[768,4096]{1,0:T(8,128)(2,1)S(1)} %get-tuple-element.18, bf16[1,4096,1536]{2,1,0:T(8,128)(2,1)} %param.20), kind=kOutput, calls=%fused_computation.7 | convolution fusion | flops 19352518656 | bytes 34603008 | tf_op jit(solution)/shard_map/dot_general | solution.py:343
  172.5 2.6 fusion.10.act
  175.1 160.7 %return_sum.1 = f32[128,4096]{1,0:T(8,128)} custom-call(bf16[1536,768]{1,0:T(8,128)(2,1)} %fusion.10.act, bf16[768,4096]{1,0:T(8,128)(2,1)} %bitcast.34, bf16[16,128,96]{2,1,0:T(8,128)(2,1)} %pad_maximum_fusion.2.wts), custom_call_target="tpu_custom_call" | custom-call | tf_op jit(solution)/shard_map/return_sum/pallas_call | solution.py:234
  335.8 0.0 copy-start.4
  335.8 2.9 multiply_reduce_fusion
  338.7 0.0 copy-done
  338.7 2.1 fusion.32
  340.9 0.0 copy-done.4
  340.9 0.1 collective-permute-start.3
  341.0 1.1 collective-permute-done.3
  342.2 0.1 reshape.74
  342.3 0.1 constant_dynamic-slice_fusion
  342.4 0.6 copy.37
  (26 shorter events, 0.3 us)
Async XLA Ops:
  7.2 331.5 %copy-start = (bf16[1,4096,28]{1,2,0:T(8,128)(2,1)S(1)}, bf16[1,4096,28]{1,2,0:T(8,128)(2,1)}, u32[]{:S(2)}) copy-start(bf16[1,4096,28]{1,2,0:T(8,128)(2,1)} %param.15) | copy-start | bytes 688132
  7.2 9.2 %copy-start.1 = (s32[128,8]{0,1:T(8,128)S(1)}, s32[128,8]{0,1:T(8,128)}, u32[]{:S(2)}) copy-start(s32[128,8]{0,1:T(8,128)} %param.16) | copy-start | bytes 12292
  7.2 119.6 %all-gather.4.cloned.1.call-start = ((), (), s32[]{:S(2)}) async-start(), calls=%async_computation | async-start | bytes 8912896 | tf_op jit(solution)/shard_map/all_gather | solution.py:272
  7.9 5.5 %collective-permute-start = (bf16[128,2048]{1,0:T(8,128)(2,1)}, bf16[128,2048]{1,0:T(8,128)(2,1)S(1)}, u32[]{:S(2)}, u32[]{:S(2)}) collective-permute-start(bf16[128,2048]{1,0:T(8,128)(2,1)} %param.11), channel_id=1, source_target_pairs={{0,16},{16,0},{1,17},{17,1},{2,18},{18,2},{3,19},{19,3},{4,20},{20... | collective-permute-start | bytes 1572872 | tf_op jit(solution)/shard_map/ppermute | solution.py:242
  126.8 13.2 %slice-start = ((s8[8388608]{0:T(1024)(128)(4,1)}), s8[4194304]{0:T(1024)(128)(4,1)S(1)}, s32[]{:S(2)}) async-start(s8[8388608]{0:T(1024)(128)(4,1)} %bitcast.30), calls=%async_computation.1 | async-start | bytes 8388608
  126.8 4.8 %copy-start.3 = (bf16[1,4096]{1,0:T(2,128)(2,1)S(1)}, bf16[1,4096]{1,0:T(2,128)(2,1)}, u32[]{:S(2)}) copy-start(bf16[1,4096]{1,0:T(2,128)(2,1)} %param.12) | copy-start | bytes 24580
  126.8 5.3 %copy-start.2 = (bf16[1,4096]{1,0:T(2,128)(2,1)S(1)}, bf16[1,4096]{1,0:T(2,128)(2,1)}, u32[]{:S(2)}) copy-start(bf16[1,4096]{1,0:T(2,128)(2,1)} %param.14) | copy-start | bytes 24580
  126.8 13.2 %slice-start.1 = ((s8[8388608]{0:T(1024)(128)(4,1)}), s8[4194304]{0:T(1024)(128)(4,1)S(1)}, s32[]{:S(2)}) async-start(s8[8388608]{0:T(1024)(128)(4,1)} %bitcast.30), calls=%async_computation.2 | async-start | bytes 8388608
  131.5 9.7 %collective-permute-start.1 = (bf16[768,2048]{1,0:T(8,128)(2,1)S(1)}, bf16[768,2048]{1,0:T(8,128)(2,1)S(1)}, u32[]{:S(2)}, u32[]{:S(2)}) collective-permute-start(bf16[768,2048]{1,0:T(8,128)(2,1)S(1)} %bitcast.33), channel_id=1, source_target_pairs={{0,16},{16,0},{1,17},{17,1},{2,18},{18,2},{3,19},{19,3},{4,20},{20... | collective-permute-start | bytes 9437192 | tf_op jit(solution)/shard_map/ppermute | solution.py:242
  131.6 5.7 %collective-permute-start.2 = (bf16[1,4096]{1,0:T(2,128)(2,1)S(1)}, bf16[1,4096]{1,0:T(2,128)(2,1)S(1)}, u32[]{:S(2)}, u32[]{:S(2)}) collective-permute-start(bf16[1,4096]{1,0:T(2,128)(2,1)S(1)} %copy-done.3), channel_id=1, source_target_pairs={{0,16},{16,0},{1,17},{17,1},{2,18},{18,2},{3,19},{19,3},{4,20},{20... | collective-permute-start | bytes 24584 | tf_op jit(solution)/shard_map/ppermute | solution.py:242
  335.8 5.1 %copy-start.4 = (s32[128,8]{0,1:T(8,128)S(1)}, s32[128,8]{0,1:T(8,128)}, u32[]{:S(2)}) copy-start(s32[128,8]{0,1:T(8,128)} %param.18) | copy-start | bytes 12292
  340.9 1.2 collective-permute-start.3
Sparse Core Ops, SparseCore 0:
  10.8 115.9 all-gather.3

commit v3 on v2

--- a/solution.py
+++ b/solution.py
@@ -237,6 +237,276 @@
     return parts[0] if len(parts) == 1 else jnp.concatenate(parts, axis=1)
 
 
+def gather_kernel(sides, chunks, x, info, gains, w_in, act, info_out, *rest):
+    (g_a, g_b, info_got, picks, scale, give, mine, got, hid, w_buf) = rest[:10]
+    sems = rest[10:]
+    n_a, n_b, n_c = sides
+    blocks = n_a * n_b * n_c
+    seg = lax.axis_index("segment")
+    me = lax.axis_index("expert")
+    a, b, c = me // (n_b * n_c), (me // n_c) % n_b, me % n_c
+    tok_rows, half = x.shape
+    part = tok_rows // 2
+    wide = half // chunks
+    slot_rows = mine.shape[1]
+    cap = slot_rows // blocks
+    tile = math.gcd(slot_rows, 256)
+    units = act.shape[1]
+    partner = (1 - seg, me)
+
+    def at(na, nb, nc):
+        return (seg, (na * n_b + nb) * n_c + nc)
+
+    def peer_a(k):
+        return at((a + k) % n_a, b, c)
+
+    def peer_b(k):
+        return at(a, (b + k) % n_b, c)
+
+    def peer_c(k):
+        return at(a, b, (c + k) % n_c)
+
+    barrier = pltpu.get_barrier_semaphore()
+    pl.semaphore_signal(barrier, inc=1, device_id=partner, device_id_type=MESH)
+
+    @pl.loop(1, blocks)
+    def _(k):
+        pl.semaphore_signal(
+            barrier, inc=1, device_id=(seg, (me + k) % blocks), device_id_type=MESH
+        )
+
+    pl.semaphore_wait(barrier, blocks)
+
+    def remote(src, dst, send, recv, peer):
+        return pltpu.make_async_remote_copy(
+            src_ref=src,
+            dst_ref=dst,
+            send_sem=send,
+            recv_sem=recv,
+            device_id=peer,
+            device_id_type=MESH,
+        )
+
+    def tell(k):
+        to = (me + k) % blocks
+        return remote(
+            info.at[to], info_got.at[me], sems[0].at[k - 1], sems[1].at[k - 1], (seg, to)
+        )
+
+    def swap(j):
+        return remote(give.at[j % 2], got.at[j], sems[2].at[j % 2], sems[3].at[j], partner)
+
+    orders = (
+        (g_a, c, b, n_c, n_b, peer_c, peer_b),
+        (g_b, b, c, n_b, n_c, peer_b, peer_c),
+    )
+
+    def columns(j):
+        return pl.ds(pl.multiple_of(j * wide, wide), wide)
+
+    def sends(which, phase, j):
+        held, outer, inner, n_outer, n_inner, peer_outer, peer_inner = orders[which]
+        send, recv = sems[5 + which * 6 + phase * 2 : 7 + which * 6 + phase * 2]
+        if phase == 0:
+            src = x.at[pl.ds(which * part, part), columns(j)]
+            dst, side, peer = held.at[j, outer, inner, a], n_a, peer_a
+        elif phase == 1:
+            src = dst = held.at[j, outer, inner]
+            side, peer = n_inner, peer_inner
+        else:
+            src = dst = held.at[j, outer]
+            side, peer = n_outer, peer_outer
+        return [
+            remote(src, dst, send.at[j % 2, k - 1], recv.at[j, k - 1], peer(k))
+            for k in range(1, side)
+        ]
+
+    def weight_copies(j):
+        copies = []
+        for which, owner in enumerate((seg, 1 - seg)):
+            rows = pl.ds(pl.multiple_of(owner * half + j * wide, wide), wide)
+            copies.append(
+                pltpu.make_async_copy(
+                    w_in.at[rows, :],
+                    w_buf.at[j % 2, pl.ds(which * wide, wide)],
+                    sems[4].at[j % 2, which],
+                )
+            )
+        return copies
+
+    def first_send(j):
+        for which in range(2):
+            held, outer, inner = orders[which][:3]
+            for copy in sends(which, 0, j):
+                copy.start()
+            held[j, outer, inner, a] = x[pl.ds(which * part, part), columns(j)]
+
+    def relay(phase, j):
+        for which in range(2):
+            for copy in sends(which, phase - 1, j):
+                copy.wait()
+            for copy in sends(which, phase, j):
+                copy.start()
+
+    def read_info():
+        info_got[me] = info[me]
+
+        @pl.loop(1, blocks)
+        def _(k):
+            tell(k).wait()
+
+        row = lax.broadcasted_iota(jnp.int32, (cap, tok_rows), 0).astype(jnp.float32)
+
+        @pl.loop(0, blocks)
+        def _(d):
+            told = info_got[d]
+            info_out[d] = told
+            own = told[0:1, :] == row
+            other = told[1:2, :] == row
+            picks[d] = jnp.concatenate(
+                [jnp.where(own, 1.0, 0.0), jnp.where(other, 1.0, 0.0)], axis=0
+            ).astype(jnp.bfloat16)
+            factor = jnp.sum(jnp.where(own, told[4:5, :], 0.0), axis=1, keepdims=True)
+            rows = pl.ds(pl.multiple_of(d * cap, cap), cap)
+            scale[rows, :] = jnp.broadcast_to(factor, (cap, wide))
+
+    def pick(j):
+        for copy in weight_copies(j):
+            copy.start()
+        for which in range(2):
+            for copy in sends(which, 2, j):
+                copy.wait()
+
+        @pl.when(j == 0)
+        def _():
+            read_info()
+
+        @pl.loop(0, blocks, unroll=4)
+        def _(d):
+            da, db, dc = d // (n_b * n_c), (d // n_c) % n_b, d % n_c
+            rows = pl.ds(pl.multiple_of(d * cap, cap), cap)
+            there = jnp.concatenate([g_a[j, dc, db, da], g_b[j, db, dc, da]], axis=0)
+            taken = jnp.dot(picks[d], there, preferred_element_type=jnp.float32)
+            taken = taken.astype(jnp.bfloat16)
+            mine[j % 2, rows, :] = taken[:cap]
+            give[j % 2, rows, :] = taken[cap:]
+
+        swap(j).start()
+
+    def multiply(j):
+        swap(j).wait()
+        for copy in weight_copies(j):
+            copy.wait()
+        places = [
+            pl.ds(pl.multiple_of(owner * half + j * wide, wide), wide) for owner in (seg, 1 - seg)
+        ]
+
+        @pl.loop(0, slot_rows // tile)
+        def _(r):
+            rows = pl.ds(pl.multiple_of(r * tile, tile), tile)
+            factor = scale[rows, :]
+            pieces = [
+                ref[rows, :].astype(jnp.float32) * factor for ref in (mine.at[j % 2], got.at[j])
+            ]
+            for section in range(2):
+                normed = jnp.concatenate(
+                    [
+                        (piece * gains[pl.ds(section, 1), place]).astype(jnp.bfloat16)
+                        for piece, place in zip(pieces, places)
+                    ],
+                    axis=1,
+                )
+                to = pl.ds(pl.multiple_of(section * slot_rows + r * tile, tile), tile)
+                hid[to, :] += jnp.dot(
+                    normed, w_buf[j % 2], preferred_element_type=jnp.float32
+                )
+
+    @pl.loop(1, blocks)
+    def _(k):
+        tell(k).start()
+
+    stages = (
+        first_send,
+        functools.partial(relay, 1),
+        functools.partial(relay, 2),
+        pick,
+        multiply,
+    )
+
+    @pl.loop(0, chunks + len(stages) - 1)
+    def _(step):
+        for lag, stage in enumerate(stages):
+
+            @pl.when((step >= lag) & (step - lag < chunks))
+            def _():
+                stage(step - lag)
+
+        @pl.when(step == 0)
+        def _():
+            @pl.loop(0, 2 * slot_rows // tile)
+            def _(r):
+                rows = pl.ds(pl.multiple_of(r * tile, tile), tile)
+                hid[rows, :] = jnp.zeros((tile, 2 * units), jnp.float32)
+
+    @pl.loop(0, 2 * slot_rows // tile)
+    def _(r):
+        rows = pl.ds(pl.multiple_of(r * tile, tile), tile)
+        gate = hid[rows, :units]
+        act[rows, :] = (gate / (1.0 + jnp.exp(-gate)) * hid[rows, units:]).astype(jnp.bfloat16)
+
+
+def gather_call(sides, room, x, info, gains, w_in):
+    n_a, n_b, n_c = sides
+    blocks = n_a * n_b * n_c
+    tok_rows, half = x.shape
+    wide = LANES
+    chunks = half // wide
+    slot_rows = blocks * room
+    units = w_in.shape[1] // 2
+    part = tok_rows // 2
+
+    def bf(*shape):
+        return pltpu.VMEM(shape, jnp.bfloat16)
+
+    def f32(*shape):
+        return pltpu.VMEM(shape, jnp.float32)
+
+    def dma(*shape):
+        return pltpu.SemaphoreType.DMA(shape)
+
+    scratch = [
+        bf(chunks, n_c, n_b, n_a, part, wide),
+        bf(chunks, n_b, n_c, n_a, part, wide),
+        f32(*info.shape),
+        bf(blocks, 2 * room, tok_rows),
+        f32(slot_rows, wide),
+        bf(2, slot_rows, wide),
+        bf(2, slot_rows, wide),
+        bf(chunks, slot_rows, wide),
+        f32(2 * slot_rows, 2 * units),
+        bf(2, 2 * wide, 2 * units),
+    ]
+    sems = [dma(blocks - 1), dma(blocks - 1), dma(2), dma(chunks), dma(2, 2)]
+    for outer, inner in ((n_c, n_b), (n_b, n_c)):
+        for side in (n_a, inner, outer):
+            sems += [dma(2, side - 1), dma(chunks, side - 1)]
+    vmem = pl.BlockSpec(memory_space=pltpu.VMEM)
+    return pl.pallas_call(
+        functools.partial(gather_kernel, sides, chunks),
+        out_shape=(
+            jax.ShapeDtypeStruct((2 * slot_rows, units), jnp.bfloat16),
+            jax.ShapeDtypeStruct(info.shape, jnp.float32),
+        ),
+        in_specs=[vmem, vmem, vmem, pl.BlockSpec(memory_space=pl.ANY)],
+        out_specs=(vmem, vmem),
+        scratch_shapes=scratch + sems,
+        compiler_params=pltpu.CompilerParams(
+            collective_id=1, has_side_effects=True, vmem_limit_bytes=60 * 1024 * 1024
+        ),
+        name="gather_hidden",
+    )(x, info, gains, w_in)
+
+
 def swap_cores(x):
     count = lax.axis_size("segment")
     return lax.ppermute(x, "segment", [(i, count - 1 - i) for i in range(count)])
@@ -267,9 +537,6 @@
     experts_all = router_first.shape[2]
     slot_count = slot_table.shape[0]
     capacity = 3 * tok_rows * top_count // (2 * segment_count * chip_count)
-    hidden_units = expert_out.shape[1]
-
-    everyone = lax.all_gather(rollout, "expert", axis=0)
 
     expert_cols = jnp.arange(experts_all, dtype=jnp.int32)
     slot_ids = jnp.arange(slot_count, dtype=jnp.int32)
@@ -285,15 +552,14 @@
     order = jnp.arange(tok_rows, dtype=jnp.int32)
     before_mask = (order[None, :] < order[:, None]).astype(jnp.bfloat16)
     before = jnp.dot(before_mask, hit, preferred_element_type=jnp.float32).astype(jnp.int32)
-    place = jnp.where(before < capacity, slot_ids * capacity + before, -1)
-    target = jnp.sum(jnp.where(match, place[:, None, :], 0), axis=-1)
     other_half = swap_cores(rollout)
     first = position == 0
     left = jnp.where(first, rollout, other_half)
     right = jnp.where(first, other_half, rollout)
     whole = jnp.concatenate([left, right], axis=1)
     states_in = whole.astype(jnp.float32)
-    normed = (states_in * inverse_rms(states_in) * norm_gain[0].astype(jnp.float32)).astype(
+    factor = inverse_rms(states_in)
+    normed = (states_in * factor * norm_gain[0].astype(jnp.float32)).astype(
         jnp.bfloat16
     )
     logits = jnp.dot(normed, router_first[0], preferred_element_type=jnp.float32)
@@ -301,55 +567,31 @@
     chosen = jnp.sum(jnp.where(picked, logits[:, None, :], 0.0), axis=-1)
     lifted = jnp.exp(chosen - jnp.max(chosen, axis=1, keepdims=True))
     gates = (lifted / jnp.sum(lifted, axis=1, keepdims=True)).astype(jnp.bfloat16)
-    packed = jnp.concatenate([target.astype(jnp.float32), gates.astype(jnp.float32)], axis=1)
-    packed = lax.all_gather(packed, "expert", axis=0)
-    targets = packed[..., :top_count].astype(jnp.int32)
-    gates_all = packed[..., top_count:]
-
-    chip = lax.axis_index("expert")
-    own_base = (position * chip_count + chip) * capacity
-    other_base = ((segment_count - 1 - position) * chip_count + chip) * capacity
-
-    def places_in(base):
-        inside = (targets >= base) & (targets < base + capacity)
-        place = jnp.sum(jnp.where(inside, targets - base + 1, 0), axis=-1) - 1
-        weight = jnp.sum(jnp.where(inside, gates_all, 0.0), axis=-1)
-        return place, weight
-
-    own_place, own_weight = places_in(own_base)
-    other_place, other_weight = places_in(other_base)
+    place = jnp.where((hit > 0) & (before < capacity), before, -1).astype(jnp.float32)
+    gate = jnp.sum(jnp.where(match, gates.astype(jnp.float32)[..., None], 0.0), axis=1)
+
+    def by_core(values):
+        cores = values.T.reshape(segment_count, chip_count, tok_rows)
+        own = jnp.where(first, cores[0], cores[1])
+        other = jnp.where(first, cores[1], cores[0])
+        return [own, other]
+
+    factors = jnp.broadcast_to(factor[:, 0], (chip_count, tok_rows))
+    blank = jnp.zeros((chip_count, tok_rows), jnp.float32)
+    info = jnp.stack(by_core(place) + by_core(gate) + [factors, blank, blank, blank], axis=1)
+    gains = jnp.concatenate([swap_cores(norm_gain), norm_gain], axis=0).astype(jnp.float32)
     room = -(-capacity // 16) * 16
-    rows = jnp.arange(room, dtype=jnp.int32)
-
-    def pick_rows(place):
-        onehot = (place[:, None, :] == rows[None, :, None]).astype(jnp.bfloat16)
-        got = jnp.einsum("sct,std->scd", onehot, everyone, preferred_element_type=jnp.float32)
-        return got.astype(jnp.bfloat16).reshape(chip_count * room, half)
-
-    other_rows = swap_cores(pick_rows(other_place))
-    own_rows = pick_rows(own_place)
-    left = jnp.where(first, own_rows, other_rows)
-    right = jnp.where(first, other_rows, own_rows)
-    full = jnp.concatenate([left, right], axis=1).astype(jnp.float32)
-    scaled = full * inverse_rms(full)
-    other_gain = swap_cores(norm_gain)
-    inputs = jnp.concatenate(
-        [
-            (scaled * gain[0].astype(jnp.float32)).astype(jnp.bfloat16)
-            for gain in (other_gain, norm_gain)
-        ],
-        axis=0,
-    )
-    hidden = jnp.dot(inputs, expert_in[0], preferred_element_type=jnp.float32)
-    active = (jax.nn.silu(hidden[:, :hidden_units]) * hidden[:, hidden_units:]).astype(jnp.bfloat16)
+    sides = grid_sides(chip_count)
+    active, told = gather_call(sides, room, rollout, info, gains, expert_in[0])
+    rows = jnp.arange(room, dtype=jnp.float32)
 
     def spread(place, weight):
         return jnp.where(place[..., None] == rows, weight[..., None], 0.0).astype(jnp.bfloat16)
 
     weights = jnp.concatenate(
-        [spread(own_place, own_weight), spread(other_place, other_weight)], axis=2
-    )
-    summed = return_call(grid_sides(chip_count), active, expert_out[0], weights)
+        [spread(told[:, 0], told[:, 2]), spread(told[:, 1], told[:, 3])], axis=2
+    )
+    summed = return_call(sides, active, expert_out[0], weights)
     mixed = states_in + summed
     later = (mixed * inverse_rms(mixed) * gain_second[0].astype(jnp.float32)).astype(jnp.bfloat16)
     logp = jax.nn.log_softmax(

time: 350 us -> 277 us (0.79)
  Pallas kernels: 161 us -> 257 us
  waiting for transfers between devices: 72.9 us -> 1.15 us
  blocking collectives: 44.3 us -> 0 us
  matrix products: 34 us -> 1.26 us
  between operations: 14.3 us -> 0.86 us
  other arithmetic: 21.7 us -> 13.1 us
    pallas_call x0 -> x1, Pallas kernels: none -> 98.3 us  [gather_call(): pl.pallas_call(functools.partial(gather_kernel, sides, chunks), out_shape...]
    all_gather x1 -> x0, waiting for transfers between devices: 65.9 us -> none  [per_device(): everyone = lax.all_gather(rollout, 'expert', axis=0)]
    all_gather x1 -> x0, blocking collectives: 44.3 us -> none  [per_device(): packed = lax.all_gather(packed, 'expert', axis=0)]
    dot_general x3 -> x0, matrix products: 30.2 us -> none  [the longest x1 24.3 us: per_device(): hidden = jnp.dot(inputs, expert_in[0], preferred_element_type=jnp.float32)]
    convert_element_type x4 -> x2, other arithmetic: 7.48 us -> 1.37 us  [the longest x1 1.36 us: per_device(): jnp.concatenate([swap_cores(norm_gain), norm_gain], axis=0)]
    ppermute x4 -> x3, waiting for transfers between devices: 6.3 us -> 1.15 us  [swap_cores(): lax.ppermute(x, 'segment', [(i, count - 1 - i) for i in range(count)])]
  transfers between devices with their start and end apart: 5 -> 3, of which waited for: 3 -> 1; matrix products, arithmetic and copies ran while one was open for 3% -> 2% of each run, Pallas kernels for 0% -> 0%
where the time goes in v3:
time: 277 us
  Pallas kernels  257 us (93%)
  other arithmetic  13.1 us (5%)
    pallas_call x1, Pallas kernels, return_call(): call(act, w_out[:, start:start + piece], wts)  159 us
    pallas_call x1, Pallas kernels, gather_call(): pl.pallas_call(functools.partial(gather_kernel, sides, chunks), out_shape...  98.3 us
  transfers between devices with their start and end apart: 3, of which 1 were waited for; matrix products, arithmetic and copies ran while one was open for 2% of the time, Pallas kernels for 0%

profile of v3, /device:TPU:0, one launch (start us, length us, event | category | flops | bytes accessed | tf_op | source)
XLA Modules:
  0.0 276.8 jit_solution(15530421804936046777)
XLA Ops:
  0.6 0.0 copy-start
  0.6 0.0 copy-start.5
  0.7 0.6 collective-permute-start
  1.2 0.1 collective-permute-start.1
  1.3 0.8 convert_reduce_fusion
  2.1 0.8 fusion.12
  2.9 0.8 add_select_fusion
  3.7 0.8 fusion.14
  4.5 0.1 select_convert_fusion.2
  4.6 0.8 mul.62
  5.4 0.7 mul.63
  6.2 0.0 collective-permute-done.1
  6.2 1.4 maximum_convert_fusion.gains
  7.5 0.0 collective-permute-done
  7.5 1.1 broadcast_select_fusion.1
  8.7 0.0 copy-start.2
  8.7 0.0 copy-start.3
  8.7 0.3 fusion
  9.0 0.0 copy-done.5
  9.0 0.5 fusion.4
  9.5 0.0 copy-done.2
  9.6 0.0 copy-done.3
  9.6 0.1 select_reduce_fusion
  9.8 0.7 stack.23.info
  10.5 98.3 %gather_hidden.1 = (bf16[1536,768]{1,0:T(8,128)(2,1)}, f32[16,8,128]{2,1,0:T(8,128)}) custom-call(bf16[128,2048]{1,0:T(8,128)(2,1)} %x.1, f32[16,8,128]{2,1,0:T(8,128)} %stack.23.info, f32[2,4096]{1,0:T(2,128)} %maximum_convert_fusion.gains, bf16[4096,1536]{1,0:T(8,128)(2,1)} %bitcast.34), custom_call_target="tpu_custom_call" | custom-call | tf_op jit(solution)/shard_map/gather_hidden/pallas_call | solution.py:494
  108.8 1.0 fusion.18
  109.9 0.6 select_convert_fusion.1
  110.5 0.6 select_convert_fusion
  111.1 1.1 pad_maximum_fusion.1.wts
  112.2 158.9 %return_sum.1 = f32[128,4096]{1,0:T(8,128)} custom-call(bf16[1536,768]{1,0:T(8,128)(2,1)} %get-tuple-element.4.act, bf16[768,4096]{1,0:T(8,128)(2,1)} %bitcast.35, bf16[16,128,96]{2,1,0:T(8,128)(2,1)} %pad_maximum_fusion.1.wts), custom_call_target="tpu_custom_call" | custom-call | tf_op jit(solution)/shard_map/return_sum/pallas_call | solution.py:234
  271.0 0.0 copy-start.1
  271.1 3.0 %multiply_reduce_fusion = (f32[128]{0:T(128)S(1)}, bf16[1,128,4096]{2,1,0:T(8,128)(2,1)}) fusion(f32[128,4096]{1,0:T(8,128)} %return_sum.1, bf16[128,2048]{1,0:T(8,128)(2,1)S(1)} %get-tuple-element.17, bf16[128,2048]{1,0:T(8,128)(2,1)S(1)} %get-tuple-element.16), kind=kLoop, calls=%fused_computation.7 | loop fusion | flops 4194176 | bytes 4194816 | tf_op jit(solution)/shard_map/reduce_sum | solution.py:516
  274.1 0.0 copy-start.4
  274.1 0.0 copy-done
  274.1 0.0 copy-done.1
  274.1 0.6 fusion.19
  274.7 0.0 copy-done.4
  274.8 0.1 collective-permute-start.2
  274.9 1.1 collective-permute-done.2
  276.0 0.1 reshape.88
  276.2 0.1 constant_dynamic-slice_fusion
  276.2 0.6 copy.36
  (15 shorter events, 0.2 us)
Async XLA Ops:
  0.6 273.4 %copy-start = (bf16[1,4096,28]{1,2,0:T(8,128)(2,1)S(1)}, bf16[1,4096,28]{1,2,0:T(8,128)(2,1)}, u32[]{:S(2)}) copy-start(bf16[1,4096,28]{1,2,0:T(8,128)(2,1)} %param.15) | copy-start | bytes 688132
  0.6 8.3 %copy-start.5 = (bf16[1,4096,28]{1,2,0:T(8,128)(2,1)S(1)}, bf16[1,4096,28]{1,2,0:T(8,128)(2,1)}, u32[]{:S(2)}) copy-start(bf16[1,4096,28]{1,2,0:T(8,128)(2,1)} %param.13) | copy-start | bytes 688132
  0.7 6.9 %collective-permute-start = (bf16[128,2048]{1,0:T(8,128)(2,1)}, bf16[128,2048]{1,0:T(8,128)(2,1)S(1)}, u32[]{:S(2)}, u32[]{:S(2)}) collective-permute-start(bf16[128,2048]{1,0:T(8,128)(2,1)} %x.1), channel_id=1, source_target_pairs={{0,16},{16,0},{1,17},{17,1},{2,18},{18,2},{3,19},{19,3},{4,20},{20... | collective-permute-start | bytes 1572872 | tf_op jit(solution)/shard_map/ppermute | solution.py:512
  1.2 4.9 %collective-permute-start.1 = (bf16[1,4096]{1,0:T(2,128)(2,1)}, bf16[1,4096]{1,0:T(2,128)(2,1)S(1)}, u32[]{:S(2)}, u32[]{:S(2)}) collective-permute-start(bf16[1,4096]{1,0:T(2,128)(2,1)} %param.12), channel_id=1, source_target_pairs={{0,16},{16,0},{1,17},{17,1},{2,18},{18,2},{3,19},{19,3},{4,20},{20... | collective-permute-start | bytes 24584 | tf_op jit(solution)/shard_map/ppermute | solution.py:512
  8.7 0.9 copy-start.2
  8.7 1.0 copy-start.3
  271.0 3.0 %copy-start.1 = (f32[128,4096]{1,0:T(8,128)S(1)}, f32[128,4096]{1,0:T(8,128)}, u32[]{:S(2)}) copy-start(f32[128,4096]{1,0:T(8,128)} %return_sum.1) | copy-start | bytes 6291460
  274.1 0.7 copy-start.4
  274.8 1.2 collective-permute-start.2

commit v4 on v3

--- a/solution.py
+++ b/solution.py
@@ -27,6 +27,7 @@
 def return_kernel(sides, chunks, act, w_out, wts, out, mine, give, got, *rest):
     n_a, n_b, n_c = sides
     bufs, sems = rest[:12], rest[12:]
+    part = out.shape[0] // 2
     seg = lax.axis_index("segment")
     me = lax.axis_index("expert")
     a, b, c = me // (n_b * n_c), (me // n_c) % n_b, me % n_c
@@ -113,17 +114,21 @@
             one(r, mine, slot_rows)
 
     def spread(j):
-        swap(j).wait()
-
-        @pl.loop(0, blocks)
+        column, turn = j // 2, j % 2
+
+        @pl.when(turn == 0)
+        def _():
+            swap(column).wait()
+
+        @pl.loop(0, blocks, unroll=4)
         def _(d):
             da, db, dc = d // (n_b * n_c), (d // n_c) % n_b, d % n_c
             rows = pl.ds(pl.multiple_of(d * cap, cap), cap)
-            both = jnp.concatenate([mine[j % 2, rows, :], got[j, rows, :]], axis=0)
-            part = jnp.dot(wts[d], both, preferred_element_type=jnp.float32)
-            part = part.astype(jnp.bfloat16)
-            bufs[0][j % 2, dc, db * n_a + da] = part[:, :half]
-            bufs[6][j % 2, db, dc * n_a + da] = part[:, half:]
+            both = jnp.concatenate([mine[column % 2, rows, :], got[column, rows, :]], axis=0)
+            given = jnp.dot(wts[turn, d], both, preferred_element_type=jnp.float32)
+            given = given.astype(jnp.bfloat16)
+            bufs[0][j % 2, dc, db * n_a + da] = given[:, :half]
+            bufs[6][j % 2, db, dc * n_a + da] = given[:, half:]
 
         for half_index in range(2):
             for copy in sends(half_index, 0, j):
@@ -171,23 +176,30 @@
             total = src[j % 2, a].astype(jnp.float32)
             for k in range(n_a - 1):
                 total += dst[j, k].astype(jnp.float32)
-            columns = pl.ds(pl.multiple_of(j * wide + half_index * half, half), half)
-            out[:, columns] = total
-
-    stages = (project, spread, first_sum, second_sum, last_sum)
-
-    @pl.loop(0, chunks + len(stages) - 1)
+            columns = pl.ds(pl.multiple_of(j // 2 * wide + half_index * half, half), half)
+            out[pl.ds(pl.multiple_of(j % 2 * part, part), part), columns] = total
+
+    stages = (
+        lambda j: pl.when(j % 2 == 0)(lambda: project(j // 2)),
+        spread,
+        first_sum,
+        second_sum,
+        last_sum,
+    )
+
+    @pl.loop(0, 2 * chunks + len(stages) - 1)
     def _(step):
         for lag, stage in enumerate(stages):
 
-            @pl.when((step >= lag) & (step - lag < chunks))
+            @pl.when((step >= lag) & (step - lag < 2 * chunks))
             def _():
                 stage(step - lag)
 
 
 def return_call(sides, act, w_out, wts):
     n_a, n_b, n_c = sides
-    tok_rows = wts.shape[1]
+    part = wts.shape[2]
+    tok_rows = 2 * part
     slot_rows = act.shape[0] // 2
     half, wide = LANES, 2 * LANES
     block_bytes = tok_rows * half * 2
@@ -209,15 +221,15 @@
     sems = [dma(2), dma(chunks)]
     for first, second in ((n_c, n_b), (n_b, n_c)):
         scratch += [
-            bf(2, first, second * n_a, tok_rows, half),
-            bf(chunks, first - 1, second * n_a, tok_rows, half),
-            bf(2, second, n_a, tok_rows, half),
-            bf(chunks, second - 1, n_a, tok_rows, half),
-            bf(2, n_a, tok_rows, half),
-            bf(chunks, n_a - 1, tok_rows, half),
+            bf(2, first, second * n_a, part, half),
+            bf(2 * chunks, first - 1, second * n_a, part, half),
+            bf(2, second, n_a, part, half),
+            bf(2 * chunks, second - 1, n_a, part, half),
+            bf(2, n_a, part, half),
+            bf(2 * chunks, n_a - 1, part, half),
         ]
         for side in (first, second, n_a):
-            sems += [dma(2, side - 1), dma(chunks, side - 1)]
+            sems += [dma(2, side - 1), dma(2 * chunks, side - 1)]
     piece = chunks * wide
     call = pl.pallas_call(
         functools.partial(return_kernel, sides, chunks),
@@ -248,6 +260,7 @@
     tok_rows, half = x.shape
     part = tok_rows // 2
     wide = half // chunks
+    pair = 2 * wide
     slot_rows = mine.shape[1]
     cap = slot_rows // blocks
     tile = math.gcd(slot_rows, 256)
@@ -324,11 +337,11 @@
     def weight_copies(j):
         copies = []
         for which, owner in enumerate((seg, 1 - seg)):
-            rows = pl.ds(pl.multiple_of(owner * half + j * wide, wide), wide)
+            rows = pl.ds(pl.multiple_of(owner * half + j * pair, pair), pair)
             copies.append(
                 pltpu.make_async_copy(
                     w_in.at[rows, :],
-                    w_buf.at[j % 2, pl.ds(which * wide, wide)],
+                    w_buf.at[j % 2, pl.ds(which * pair, pair)],
                     sems[4].at[j % 2, which],
                 )
             )
@@ -368,14 +381,20 @@
             ).astype(jnp.bfloat16)
             factor = jnp.sum(jnp.where(own, told[4:5, :], 0.0), axis=1, keepdims=True)
             rows = pl.ds(pl.multiple_of(d * cap, cap), cap)
-            scale[rows, :] = jnp.broadcast_to(factor, (cap, wide))
+            scale[rows, :] = jnp.broadcast_to(factor, (cap, pair))
+
+    def settle(j):
+        for which in range(2):
+            for copy in sends(which, 2, j):
+                copy.wait()
+
+        @pl.when(j % 2 == 1)
+        def _():
+            pick(j // 2)
 
     def pick(j):
         for copy in weight_copies(j):
             copy.start()
-        for which in range(2):
-            for copy in sends(which, 2, j):
-                copy.wait()
 
         @pl.when(j == 0)
         def _():
@@ -385,7 +404,13 @@
         def _(d):
             da, db, dc = d // (n_b * n_c), (d // n_c) % n_b, d % n_c
             rows = pl.ds(pl.multiple_of(d * cap, cap), cap)
-            there = jnp.concatenate([g_a[j, dc, db, da], g_b[j, db, dc, da]], axis=0)
+            there = jnp.concatenate(
+                [
+                    jnp.concatenate([g_a[i, dc, db, da], g_b[i, db, dc, da]], axis=0)
+                    for i in (2 * j, 2 * j + 1)
+                ],
+                axis=1,
+            )
             taken = jnp.dot(picks[d], there, preferred_element_type=jnp.float32)
             taken = taken.astype(jnp.bfloat16)
             mine[j % 2, rows, :] = taken[:cap]
@@ -398,7 +423,7 @@
         for copy in weight_copies(j):
             copy.wait()
         places = [
-            pl.ds(pl.multiple_of(owner * half + j * wide, wide), wide) for owner in (seg, 1 - seg)
+            pl.ds(pl.multiple_of(owner * half + j * pair, pair), pair) for owner in (seg, 1 - seg)
         ]
 
         @pl.loop(0, slot_rows // tile)
@@ -429,8 +454,8 @@
         first_send,
         functools.partial(relay, 1),
         functools.partial(relay, 2),
-        pick,
-        multiply,
+        settle,
+        lambda j: pl.when(j % 2 == 1)(lambda: multiply(j // 2)),
     )
 
     @pl.loop(0, chunks + len(stages) - 1)
@@ -479,14 +504,14 @@
         bf(chunks, n_b, n_c, n_a, part, wide),
         f32(*info.shape),
         bf(blocks, 2 * room, tok_rows),
-        f32(slot_rows, wide),
-        bf(2, slot_rows, wide),
-        bf(2, slot_rows, wide),
-        bf(chunks, slot_rows, wide),
+        f32(slot_rows, 2 * wide),
+        bf(2, slot_rows, 2 * wide),
+        bf(2, slot_rows, 2 * wide),
+        bf(chunks // 2, slot_rows, 2 * wide),
         f32(2 * slot_rows, 2 * units),
-        bf(2, 2 * wide, 2 * units),
+        bf(2, 4 * wide, 2 * units),
     ]
-    sems = [dma(blocks - 1), dma(blocks - 1), dma(2), dma(chunks), dma(2, 2)]
+    sems = [dma(blocks - 1), dma(blocks - 1), dma(2), dma(chunks // 2), dma(2, 2)]
     for outer, inner in ((n_c, n_b), (n_b, n_c)):
         for side in (n_a, inner, outer):
             sems += [dma(2, side - 1), dma(chunks, side - 1)]
@@ -591,6 +616,7 @@
     weights = jnp.concatenate(
         [spread(told[:, 0], told[:, 2]), spread(told[:, 1], told[:, 3])], axis=2
     )
+    weights = weights.reshape(chip_count, 2, tok_rows // 2, 2 * room).transpose(1, 0, 2, 3)
     summed = return_call(sides, active, expert_out[0], weights)
     mixed = states_in + summed
     later = (mixed * inverse_rms(mixed) * gain_second[0].astype(jnp.float32)).astype(jnp.bfloat16)

time: 277 us -> 288 us (1.040)
  Pallas kernels: 257 us -> 267 us
    pallas_call x1, Pallas kernels: 159 us -> 166 us  [return_call(): call(act, w_out[:, start:start + piece], wts)]
    pallas_call x1, Pallas kernels: 98.3 us -> 102 us  [gather_call(): pl.pallas_call(functools.partial(gather_kernel, sides, chunks), out_shape...]
where the time goes in v4:
time: 288 us; the launch traced here: 287 us
  Pallas kernels  267 us (93%)
  other arithmetic  13.1 us (5%)
  local copies, waits for them, and re-layouts  3.02 us (1%)
    pallas_call x1, Pallas kernels, return_call(): call(act, w_out[:, start:start + piece], wts)  166 us
    pallas_call x1, Pallas kernels, gather_call(): pl.pallas_call(functools.partial(gather_kernel, sides, chunks), out_shape...  102 us
  transfers between devices with their start and end apart: 3, of which 1 were waited for; matrix products, arithmetic and copies ran while one was open for 2% of the time, Pallas kernels for 0%

profile of v4, /device:TPU:0, one launch (start us, length us, event | category | flops | bytes accessed | tf_op | source)
XLA Modules:
  0.0 287.3 jit_solution(767760961605913314)
XLA Ops:
  0.6 0.0 copy-start
  0.6 0.0 copy-start.5
  0.7 0.6 collective-permute-start
  1.2 0.1 collective-permute-start.1
  1.3 0.8 convert_reduce_fusion
  2.1 0.8 fusion.12
  2.9 0.8 add_select_fusion
  3.7 0.8 fusion.14
  4.5 0.1 select_convert_fusion.2
  4.6 0.8 mul.62
  5.4 0.7 mul.63
  6.2 0.0 collective-permute-done.1
  6.2 1.4 maximum_convert_fusion.gains
  7.5 0.0 collective-permute-done
  7.5 1.1 broadcast_select_fusion.1
  8.7 0.0 copy-start.2
  8.7 0.0 copy-start.3
  8.7 0.3 fusion
  9.0 0.0 copy-done.5
  9.0 0.5 fusion.4
  9.5 0.0 copy-done.2
  9.6 0.0 copy-done.3
  9.6 0.1 select_reduce_fusion
  9.8 0.7 stack.23.info
  10.5 101.5 %gather_hidden.1 = (bf16[1536,768]{1,0:T(8,128)(2,1)}, f32[16,8,128]{2,1,0:T(8,128)}) custom-call(bf16[128,2048]{1,0:T(8,128)(2,1)} %x.1, f32[16,8,128]{2,1,0:T(8,128)} %stack.23.info, f32[2,4096]{1,0:T(2,128)} %maximum_convert_fusion.gains, bf16[4096,1536]{1,0:T(8,128)(2,1)} %bitcast.32), custom_call_target="tpu_custom_call" | custom-call | tf_op jit(solution)/shard_map/gather_hidden/pallas_call | solution.py:519
  112.1 1.1 slice_reduce_fusion.3
  113.2 0.1 eq.121
  113.2 0.1 broadcast_in_dim.108
  113.3 0.1 eq.125
  113.4 0.1 broadcast_in_dim.111
  113.5 0.6 select_convert_fusion.1
  114.1 0.6 select_convert_fusion
  114.7 1.1 maximum_bitcast_fusion.wts
  115.8 165.7 %return_sum.1 = f32[128,4096]{1,0:T(8,128)} custom-call(bf16[1536,768]{1,0:T(8,128)(2,1)} %get-tuple-element.4.act, bf16[768,4096]{1,0:T(8,128)(2,1)} %bitcast.33, bf16[2,16,64,96]{3,2,1,0:T(8,128)(2,1)} %maximum_bitcast_fusion.wts), custom_call_target="tpu_custom_call" | custom-call | tf_op jit(solution)/shard_map/return_sum/pallas_call | solution.py:246
  281.6 0.0 copy-start.1
  281.6 3.0 %multiply_reduce_fusion = (f32[128]{0:T(128)S(1)}, bf16[1,128,4096]{2,1,0:T(8,128)(2,1)}) fusion(f32[128,4096]{1,0:T(8,128)} %return_sum.1, bf16[128,2048]{1,0:T(8,128)(2,1)S(1)} %get-tuple-element.21, bf16[128,2048]{1,0:T(8,128)(2,1)S(1)} %get-tuple-element.20), kind=kLoop, calls=%fused_computation.7 | loop fusion | flops 4194176 | bytes 4194816 | tf_op jit(solution)/shard_map/reduce_sum | solution.py:541
  284.6 0.0 copy-start.4
  284.6 0.0 copy-done
  284.6 0.0 copy-done.1
  284.6 0.6 fusion.18
  285.2 0.0 copy-done.4
  285.3 0.1 collective-permute-start.2
  285.4 1.1 collective-permute-done.2
  286.5 0.1 reshape.99
  286.7 0.1 constant_dynamic-slice_fusion
  286.8 0.6 copy.48
  (19 shorter events, 0.3 us)
Async XLA Ops:
  0.6 284.0 %copy-start = (bf16[1,4096,28]{1,2,0:T(8,128)(2,1)S(1)}, bf16[1,4096,28]{1,2,0:T(8,128)(2,1)}, u32[]{:S(2)}) copy-start(bf16[1,4096,28]{1,2,0:T(8,128)(2,1)} %param.15) | copy-start | bytes 688132
  0.6 8.3 %copy-start.5 = (bf16[1,4096,28]{1,2,0:T(8,128)(2,1)S(1)}, bf16[1,4096,28]{1,2,0:T(8,128)(2,1)}, u32[]{:S(2)}) copy-start(bf16[1,4096,28]{1,2,0:T(8,128)(2,1)} %param.13) | copy-start | bytes 688132
  0.7 6.9 %collective-permute-start = (bf16[128,2048]{1,0:T(8,128)(2,1)}, bf16[128,2048]{1,0:T(8,128)(2,1)S(1)}, u32[]{:S(2)}, u32[]{:S(2)}) collective-permute-start(bf16[128,2048]{1,0:T(8,128)(2,1)} %x.1), channel_id=1, source_target_pairs={{0,16},{16,0},{1,17},{17,1},{2,18},{18,2},{3,19},{19,3},{4,20},{20... | collective-permute-start | bytes 1572872 | tf_op jit(solution)/shard_map/ppermute | solution.py:537
  1.2 4.9 %collective-permute-start.1 = (bf16[1,4096]{1,0:T(2,128)(2,1)}, bf16[1,4096]{1,0:T(2,128)(2,1)S(1)}, u32[]{:S(2)}, u32[]{:S(2)}) collective-permute-start(bf16[1,4096]{1,0:T(2,128)(2,1)} %param.12), channel_id=1, source_target_pairs={{0,16},{16,0},{1,17},{17,1},{2,18},{18,2},{3,19},{19,3},{4,20},{20... | collective-permute-start | bytes 24584 | tf_op jit(solution)/shard_map/ppermute | solution.py:537
  8.7 0.9 copy-start.2
  8.7 1.0 copy-start.3
  281.6 3.0 %copy-start.1 = (f32[128,4096]{1,0:T(8,128)S(1)}, f32[128,4096]{1,0:T(8,128)}, u32[]{:S(2)}) copy-start(f32[128,4096]{1,0:T(8,128)} %return_sum.1) | copy-start | bytes 6291460
  284.6 0.7 copy-start.4
  285.3 1.2 collective-permute-start.2

commit v5 on v3

--- a/solution.py
+++ b/solution.py
@@ -9,6 +9,7 @@
 from jax.sharding import PartitionSpec as P
 
 LANES = 128
+DEPTH = 3
 VMEM_BUDGET = 24 << 20
 MESH = pl.DeviceIdType.MESH
 
@@ -82,9 +83,9 @@
         place, side, peer = (first, second, (a, n_a, peer_a))[phase]
         return [
             pltpu.make_async_remote_copy(
-                src_ref=src.at[j % 2, (place + k) % side],
+                src_ref=src.at[j % DEPTH, (place + k) % side],
                 dst_ref=dst.at[j, k - 1],
-                send_sem=send.at[j % 2, k - 1],
+                send_sem=send.at[j % DEPTH, k - 1],
                 recv_sem=recv.at[j, k - 1],
                 device_id=peer(k),
                 device_id_type=MESH,
@@ -122,8 +123,8 @@
             both = jnp.concatenate([mine[j % 2, rows, :], got[j, rows, :]], axis=0)
             part = jnp.dot(wts[d], both, preferred_element_type=jnp.float32)
             part = part.astype(jnp.bfloat16)
-            bufs[0][j % 2, dc, db * n_a + da] = part[:, :half]
-            bufs[6][j % 2, db, dc * n_a + da] = part[:, half:]
+            bufs[0][j % DEPTH, dc, db * n_a + da] = part[:, :half]
+            bufs[6][j % DEPTH, db, dc * n_a + da] = part[:, half:]
 
         for half_index in range(2):
             for copy in sends(half_index, 0, j):
@@ -138,10 +139,10 @@
 
             @pl.loop(0, side2 * n_a)
             def _(d):
-                total = src[j % 2, place, d].astype(jnp.float32)
+                total = src[j % DEPTH, place, d].astype(jnp.float32)
                 for k in range(side - 1):
                     total += dst[j, k, d].astype(jnp.float32)
-                nxt[j % 2, d // n_a, d % n_a] = total.astype(jnp.bfloat16)
+                nxt[j % DEPTH, d // n_a, d % n_a] = total.astype(jnp.bfloat16)
 
             for copy in sends(half_index, 1, j):
                 copy.start()
@@ -155,10 +156,10 @@
 
             @pl.loop(0, n_a)
             def _(d):
-                total = src[j % 2, place, d].astype(jnp.float32)
+                total = src[j % DEPTH, place, d].astype(jnp.float32)
                 for k in range(side - 1):
                     total += dst[j, k, d].astype(jnp.float32)
-                nxt[j % 2, d] = total.astype(jnp.bfloat16)
+                nxt[j % DEPTH, d] = total.astype(jnp.bfloat16)
 
             for copy in sends(half_index, 2, j):
                 copy.start()
@@ -168,17 +169,17 @@
             src, dst = bufs[half_index * 6 + 4 : half_index * 6 + 6]
             for copy in sends(half_index, 2, j):
                 copy.wait()
-            total = src[j % 2, a].astype(jnp.float32)
+            total = src[j % DEPTH, a].astype(jnp.float32)
             for k in range(n_a - 1):
                 total += dst[j, k].astype(jnp.float32)
             columns = pl.ds(pl.multiple_of(j * wide + half_index * half, half), half)
             out[:, columns] = total
 
-    stages = (project, spread, first_sum, second_sum, last_sum)
-
-    @pl.loop(0, chunks + len(stages) - 1)
+    stages = ((0, project), (1, spread), (3, first_sum), (5, second_sum), (7, last_sum))
+
+    @pl.loop(0, chunks + stages[-1][0])
     def _(step):
-        for lag, stage in enumerate(stages):
+        for lag, stage in stages:
 
             @pl.when((step >= lag) & (step - lag < chunks))
             def _():
@@ -209,15 +210,15 @@
     sems = [dma(2), dma(chunks)]
     for first, second in ((n_c, n_b), (n_b, n_c)):
         scratch += [
-            bf(2, first, second * n_a, tok_rows, half),
+            bf(DEPTH, first, second * n_a, tok_rows, half),
             bf(chunks, first - 1, second * n_a, tok_rows, half),
-            bf(2, second, n_a, tok_rows, half),
+            bf(DEPTH, second, n_a, tok_rows, half),
             bf(chunks, second - 1, n_a, tok_rows, half),
-            bf(2, n_a, tok_rows, half),
+            bf(DEPTH, n_a, tok_rows, half),
             bf(chunks, n_a - 1, tok_rows, half),
         ]
         for side in (first, second, n_a):
-            sems += [dma(2, side - 1), dma(chunks, side - 1)]
+            sems += [dma(DEPTH, side - 1), dma(chunks, side - 1)]
     piece = chunks * wide
     call = pl.pallas_call(
         functools.partial(return_kernel, sides, chunks),
@@ -317,7 +318,7 @@
             src = dst = held.at[j, outer]
             side, peer = n_outer, peer_outer
         return [
-            remote(src, dst, send.at[j % 2, k - 1], recv.at[j, k - 1], peer(k))
+            remote(src, dst, send.at[j % DEPTH, k - 1], recv.at[j, k - 1], peer(k))
             for k in range(1, side)
         ]
 
@@ -426,16 +427,16 @@
         tell(k).start()
 
     stages = (
-        first_send,
-        functools.partial(relay, 1),
-        functools.partial(relay, 2),
-        pick,
-        multiply,
-    )
-
-    @pl.loop(0, chunks + len(stages) - 1)
+        (0, first_send),
+        (2, functools.partial(relay, 1)),
+        (4, functools.partial(relay, 2)),
+        (6, pick),
+        (7, multiply),
+    )
+
+    @pl.loop(0, chunks + stages[-1][0])
     def _(step):
-        for lag, stage in enumerate(stages):
+        for lag, stage in stages:
 
             @pl.when((step >= lag) & (step - lag < chunks))
             def _():
@@ -489,7 +490,7 @@
     sems = [dma(blocks - 1), dma(blocks - 1), dma(2), dma(chunks), dma(2, 2)]
     for outer, inner in ((n_c, n_b), (n_b, n_c)):
         for side in (n_a, inner, outer):
-            sems += [dma(2, side - 1), dma(chunks, side - 1)]
+            sems += [dma(DEPTH, side - 1), dma(chunks, side - 1)]
     vmem = pl.BlockSpec(memory_space=pltpu.VMEM)
     return pl.pallas_call(
         functools.partial(gather_kernel, sides, chunks),

time: 277 us -> 280 us (1.011)
    pallas_call x1, Pallas kernels: 159 us -> 163 us  [return_call(): call(act, w_out[:, start:start + piece], wts)]
where the time goes in v5:
time: 280 us; the launch traced here: 279 us
  Pallas kernels  259 us (92%)
  other arithmetic  13.1 us (5%)
    pallas_call x1, Pallas kernels, return_call(): call(act, w_out[:, start:start + piece], wts)  163 us
    pallas_call x1, Pallas kernels, gather_call(): pl.pallas_call(functools.partial(gather_kernel, sides, chunks), out_shape...  96.8 us
  transfers between devices with their start and end apart: 3, of which 1 were waited for; matrix products, arithmetic and copies ran while one was open for 2% of the time, Pallas kernels for 0%

profile of v5, /device:TPU:0, one launch (start us, length us, event | category | flops | bytes accessed | tf_op | source)
XLA Modules:
  0.0 279.1 jit_solution(2701071414772314825)
XLA Ops:
  0.6 0.0 copy-start
  0.6 0.0 copy-start.5
  0.7 0.6 collective-permute-start
  1.2 0.1 collective-permute-start.1
  1.3 0.8 convert_reduce_fusion
  2.1 0.8 fusion.12
  2.9 0.8 add_select_fusion
  3.7 0.8 fusion.14
  4.5 0.1 select_convert_fusion.2
  4.6 0.8 mul.62
  5.4 0.7 mul.63
  6.2 0.0 collective-permute-done.1
  6.2 1.4 maximum_convert_fusion.gains
  7.5 0.0 collective-permute-done
  7.5 1.1 broadcast_select_fusion.1
  8.7 0.0 copy-start.2
  8.7 0.0 copy-start.3
  8.7 0.3 fusion
  9.0 0.0 copy-done.5
  9.0 0.5 fusion.4
  9.5 0.0 copy-done.2
  9.6 0.0 copy-done.3
  9.6 0.1 select_reduce_fusion
  9.8 0.7 stack.23.info
  10.5 96.8 %gather_hidden.1 = (bf16[1536,768]{1,0:T(8,128)(2,1)}, f32[16,8,128]{2,1,0:T(8,128)}) custom-call(bf16[128,2048]{1,0:T(8,128)(2,1)} %x.1, f32[16,8,128]{2,1,0:T(8,128)} %stack.23.info, f32[2,4096]{1,0:T(2,128)} %maximum_convert_fusion.gains, bf16[4096,1536]{1,0:T(8,128)(2,1)} %bitcast.34), custom_call_target="tpu_custom_call" | custom-call | tf_op jit(solution)/shard_map/gather_hidden/pallas_call | solution.py:495
  107.4 1.0 fusion.18
  108.4 0.6 select_convert_fusion.1
  109.0 0.6 select_convert_fusion
  109.6 1.1 pad_maximum_fusion.1.wts
  110.7 162.6 %return_sum.1 = f32[128,4096]{1,0:T(8,128)} custom-call(bf16[1536,768]{1,0:T(8,128)(2,1)} %get-tuple-element.4.act, bf16[768,4096]{1,0:T(8,128)(2,1)} %bitcast.35, bf16[16,128,96]{2,1,0:T(8,128)(2,1)} %pad_maximum_fusion.1.wts), custom_call_target="tpu_custom_call" | custom-call | tf_op jit(solution)/shard_map/return_sum/pallas_call | solution.py:235
  273.3 0.0 copy-start.1
  273.3 3.0 %multiply_reduce_fusion = (f32[128]{0:T(128)S(1)}, bf16[1,128,4096]{2,1,0:T(8,128)(2,1)}) fusion(f32[128,4096]{1,0:T(8,128)} %return_sum.1, bf16[128,2048]{1,0:T(8,128)(2,1)S(1)} %get-tuple-element.17, bf16[128,2048]{1,0:T(8,128)(2,1)S(1)} %get-tuple-element.16), kind=kLoop, calls=%fused_computation.7 | loop fusion | flops 4194176 | bytes 4194816 | tf_op jit(solution)/shard_map/reduce_sum | solution.py:517
  276.3 0.0 copy-start.4
  276.3 0.0 copy-done
  276.3 0.0 copy-done.1
  276.4 0.6 fusion.19
  277.0 0.0 copy-done.4
  277.1 0.1 collective-permute-start.2
  277.1 1.1 collective-permute-done.2
  278.3 0.1 reshape.88
  278.4 0.1 constant_dynamic-slice_fusion
  278.5 0.6 copy.36
  (15 shorter events, 0.2 us)
Async XLA Ops:
  0.6 275.7 %copy-start = (bf16[1,4096,28]{1,2,0:T(8,128)(2,1)S(1)}, bf16[1,4096,28]{1,2,0:T(8,128)(2,1)}, u32[]{:S(2)}) copy-start(bf16[1,4096,28]{1,2,0:T(8,128)(2,1)} %param.15) | copy-start | bytes 688132
  0.6 8.3 %copy-start.5 = (bf16[1,4096,28]{1,2,0:T(8,128)(2,1)S(1)}, bf16[1,4096,28]{1,2,0:T(8,128)(2,1)}, u32[]{:S(2)}) copy-start(bf16[1,4096,28]{1,2,0:T(8,128)(2,1)} %param.13) | copy-start | bytes 688132
  0.7 6.9 %collective-permute-start = (bf16[128,2048]{1,0:T(8,128)(2,1)}, bf16[128,2048]{1,0:T(8,128)(2,1)S(1)}, u32[]{:S(2)}, u32[]{:S(2)}) collective-permute-start(bf16[128,2048]{1,0:T(8,128)(2,1)} %x.1), channel_id=1, source_target_pairs={{0,16},{16,0},{1,17},{17,1},{2,18},{18,2},{3,19},{19,3},{4,20},{20... | collective-permute-start | bytes 1572872 | tf_op jit(solution)/shard_map/ppermute | solution.py:513
  1.2 4.9 %collective-permute-start.1 = (bf16[1,4096]{1,0:T(2,128)(2,1)}, bf16[1,4096]{1,0:T(2,128)(2,1)S(1)}, u32[]{:S(2)}, u32[]{:S(2)}) collective-permute-start(bf16[1,4096]{1,0:T(2,128)(2,1)} %param.12), channel_id=1, source_target_pairs={{0,16},{16,0},{1,17},{17,1},{2,18},{18,2},{3,19},{19,3},{4,20},{20... | collective-permute-start | bytes 24584 | tf_op jit(solution)/shard_map/ppermute | solution.py:513
  8.7 0.9 copy-start.2
  8.7 1.0 copy-start.3
  273.3 3.0 %copy-start.1 = (f32[128,4096]{1,0:T(8,128)S(1)}, f32[128,4096]{1,0:T(8,128)}, u32[]{:S(2)}) copy-start(f32[128,4096]{1,0:T(8,128)} %return_sum.1) | copy-start | bytes 6291460
  276.3 0.7 copy-start.4
  277.1 1.2 collective-permute-start.2

commit v6 on v3

--- a/solution.py
+++ b/solution.py
@@ -304,12 +304,17 @@
     def columns(j):
         return pl.ds(pl.multiple_of(j * wide, wide), wide)
 
-    def sends(which, phase, j):
+    def sends(which, phase, j, turned=False):
         held, outer, inner, n_outer, n_inner, peer_outer, peer_inner = orders[which]
         send, recv = sems[5 + which * 6 + phase * 2 : 7 + which * 6 + phase * 2]
         if phase == 0:
             src = x.at[pl.ds(which * part, part), columns(j)]
             dst, side, peer = held.at[j, outer, inner, a], n_a, peer_a
+            if turned:
+                side, peer = n_inner, peer_inner
+        elif phase == 1 and turned:
+            src = dst = held.at[j, outer, :, a]
+            side, peer = n_a, peer_a
         elif phase == 1:
             src = dst = held.at[j, outer, inner]
             side, peer = n_inner, peer_inner
@@ -334,19 +339,24 @@
             )
         return copies
 
+    def each(which, phase, j, action):
+        for turned in (False, True):
+
+            @pl.when(j % 3 == 2 if turned else j % 3 != 2)
+            def _():
+                for copy in sends(which, phase, j, turned):
+                    action(copy)
+
     def first_send(j):
         for which in range(2):
             held, outer, inner = orders[which][:3]
-            for copy in sends(which, 0, j):
-                copy.start()
+            each(which, 0, j, lambda copy: copy.start())
             held[j, outer, inner, a] = x[pl.ds(which * part, part), columns(j)]
 
     def relay(phase, j):
         for which in range(2):
-            for copy in sends(which, phase - 1, j):
-                copy.wait()
-            for copy in sends(which, phase, j):
-                copy.start()
+            each(which, phase - 1, j, lambda copy: copy.wait())
+            each(which, phase, j, lambda copy: copy.start())
 
     def read_info():
         info_got[me] = info[me]
@@ -488,7 +498,7 @@
     ]
     sems = [dma(blocks - 1), dma(blocks - 1), dma(2), dma(chunks), dma(2, 2)]
     for outer, inner in ((n_c, n_b), (n_b, n_c)):
-        for side in (n_a, inner, outer):
+        for side in (max(n_a, inner), max(n_a, inner), outer):
             sems += [dma(2, side - 1), dma(chunks, side - 1)]
     vmem = pl.BlockSpec(memory_space=pltpu.VMEM)
     return pl.pallas_call(

time: 277 us -> 287 us (1.036)
  Pallas kernels: 257 us -> 267 us
    pallas_call x1, Pallas kernels: 98.3 us -> 107 us  [gather_call(): pl.pallas_call(functools.partial(gather_kernel, sides, chunks), out_shape...]
where the time goes in v6:
time: 287 us; the launch traced here: 286 us
  Pallas kernels  267 us (93%)
  other arithmetic  13.1 us (5%)
    pallas_call x1, Pallas kernels, return_call(): call(act, w_out[:, start:start + piece], wts)  159 us
    pallas_call x1, Pallas kernels, gather_call(): pl.pallas_call(functools.partial(gather_kernel, sides, chunks), out_shape...  107 us
  transfers between devices with their start and end apart: 3, of which 1 were waited for; matrix products, arithmetic and copies ran while one was open for 2% of the time, Pallas kernels for 0%

profile of v6, /device:TPU:0, one launch (start us, length us, event | category | flops | bytes accessed | tf_op | source)
XLA Modules:
  0.0 286.5 jit_solution(1843340408244836571)
XLA Ops:
  0.6 0.0 copy-start
  0.6 0.0 copy-start.5
  0.7 0.6 collective-permute-start
  1.2 0.1 collective-permute-start.1
  1.3 0.8 convert_reduce_fusion
  2.1 0.8 fusion.12
  2.9 0.8 add_select_fusion
  3.7 0.8 fusion.14
  4.5 0.1 select_convert_fusion.2
  4.6 0.8 mul.62
  5.4 0.7 mul.63
  6.2 0.0 collective-permute-done.1
  6.2 1.4 maximum_convert_fusion.gains
  7.5 0.0 collective-permute-done
  7.5 1.1 broadcast_select_fusion.1
  8.7 0.0 copy-start.2
  8.7 0.0 copy-start.3
  8.7 0.3 fusion
  9.0 0.0 copy-done.5
  9.0 0.5 fusion.4
  9.5 0.0 copy-done.2
  9.6 0.0 copy-done.3
  9.6 0.1 select_reduce_fusion
  9.8 0.7 stack.23.info
  10.5 107.4 %gather_hidden.1 = (bf16[1536,768]{1,0:T(8,128)(2,1)}, f32[16,8,128]{2,1,0:T(8,128)}) custom-call(bf16[128,2048]{1,0:T(8,128)(2,1)} %x.1, f32[16,8,128]{2,1,0:T(8,128)} %stack.23.info, f32[2,4096]{1,0:T(2,128)} %maximum_convert_fusion.gains, bf16[4096,1536]{1,0:T(8,128)(2,1)} %bitcast.34), custom_call_target="tpu_custom_call" | custom-call | tf_op jit(solution)/shard_map/gather_hidden/pallas_call | solution.py:504
  117.9 1.0 fusion.18
  118.9 0.6 select_convert_fusion.1
  119.5 0.6 select_convert_fusion
  120.1 1.1 pad_maximum_fusion.1.wts
  121.2 159.4 %return_sum.1 = f32[128,4096]{1,0:T(8,128)} custom-call(bf16[1536,768]{1,0:T(8,128)(2,1)} %get-tuple-element.4.act, bf16[768,4096]{1,0:T(8,128)(2,1)} %bitcast.35, bf16[16,128,96]{2,1,0:T(8,128)(2,1)} %pad_maximum_fusion.1.wts), custom_call_target="tpu_custom_call" | custom-call | tf_op jit(solution)/shard_map/return_sum/pallas_call | solution.py:234
  280.7 0.0 copy-start.1
  280.7 3.0 %multiply_reduce_fusion = (f32[128]{0:T(128)S(1)}, bf16[1,128,4096]{2,1,0:T(8,128)(2,1)}) fusion(f32[128,4096]{1,0:T(8,128)} %return_sum.1, bf16[128,2048]{1,0:T(8,128)(2,1)S(1)} %get-tuple-element.17, bf16[128,2048]{1,0:T(8,128)(2,1)S(1)} %get-tuple-element.16), kind=kLoop, calls=%fused_computation.7 | loop fusion | flops 4194176 | bytes 4194816 | tf_op jit(solution)/shard_map/reduce_sum | solution.py:526
  283.7 0.0 copy-start.4
  283.7 0.0 copy-done
  283.7 0.0 copy-done.1
  283.7 0.6 fusion.19
  284.4 0.0 copy-done.4
  284.4 0.1 collective-permute-start.2
  284.5 1.1 collective-permute-done.2
  285.6 0.1 reshape.88
  285.8 0.1 constant_dynamic-slice_fusion
  285.9 0.6 copy.36
  (15 shorter events, 0.2 us)
Async XLA Ops:
  0.6 283.1 %copy-start = (bf16[1,4096,28]{1,2,0:T(8,128)(2,1)S(1)}, bf16[1,4096,28]{1,2,0:T(8,128)(2,1)}, u32[]{:S(2)}) copy-start(bf16[1,4096,28]{1,2,0:T(8,128)(2,1)} %param.15) | copy-start | bytes 688132
  0.6 8.3 %copy-start.5 = (bf16[1,4096,28]{1,2,0:T(8,128)(2,1)S(1)}, bf16[1,4096,28]{1,2,0:T(8,128)(2,1)}, u32[]{:S(2)}) copy-start(bf16[1,4096,28]{1,2,0:T(8,128)(2,1)} %param.13) | copy-start | bytes 688132
  0.7 6.9 %collective-permute-start = (bf16[128,2048]{1,0:T(8,128)(2,1)}, bf16[128,2048]{1,0:T(8,128)(2,1)S(1)}, u32[]{:S(2)}, u32[]{:S(2)}) collective-permute-start(bf16[128,2048]{1,0:T(8,128)(2,1)} %x.1), channel_id=1, source_target_pairs={{0,16},{16,0},{1,17},{17,1},{2,18},{18,2},{3,19},{19,3},{4,20},{20... | collective-permute-start | bytes 1572872 | tf_op jit(solution)/shard_map/ppermute | solution.py:522
  1.2 4.9 %collective-permute-start.1 = (bf16[1,4096]{1,0:T(2,128)(2,1)}, bf16[1,4096]{1,0:T(2,128)(2,1)S(1)}, u32[]{:S(2)}, u32[]{:S(2)}) collective-permute-start(bf16[1,4096]{1,0:T(2,128)(2,1)} %param.12), channel_id=1, source_target_pairs={{0,16},{16,0},{1,17},{17,1},{2,18},{18,2},{3,19},{19,3},{4,20},{20... | collective-permute-start | bytes 24584 | tf_op jit(solution)/shard_map/ppermute | solution.py:522
  8.7 0.9 copy-start.2
  8.7 1.0 copy-start.3
  280.7 3.0 %copy-start.1 = (f32[128,4096]{1,0:T(8,128)S(1)}, f32[128,4096]{1,0:T(8,128)}, u32[]{:S(2)}) copy-start(f32[128,4096]{1,0:T(8,128)} %return_sum.1) | copy-start | bytes 6291460
  283.7 0.7 copy-start.4
  284.4 1.2 collective-permute-start.2
